TPU v7x, 128 devices: a whole 4x4x4 slice. The times are simulated.
128 devices in a mesh: own: 8 (over y_lo, x), dp: 16 (over y_hi, z, core).
Axes of the slice: x: 4, y: 4 (y_hi: 2, y_lo: 2; y = y_hi * 2 + y_lo), z: 4, core: 2. Of those that a mesh axis runs over, the one named last changes fastest.
Arguments:
- tokens: bfloat16 [16384, 1536], P('dp'), may hold values from -6 to 6
- assign: int32 [128, 2], P('dp'), may hold values from 0 to 7, all different within a row; in each aligned block of 8 rows (0 to 7, 8 to 15, ...) at most 5 rows name the same one
- gates: float32 [16384, 2], P('dp'), may hold values from 0.25 to 1
- cot: bfloat16 [16384, 1536], P('dp', 'own'), may hold values from -1.75 to 1.75
- w_in: bfloat16 [8, 1536, 2048], P('own', None, 'dp'), may hold values from -0.15625 to 0.15625
- w_out: bfloat16 [8, 2048, 1536], P('own', 'dp'), may hold values from -0.125 to 0.125
Outputs:
- mixed: bfloat16 [16384, 1536], P('dp', 'own')
- grad_tokens: bfloat16 [16384, 1536], P('dp', 'own')
- grad_w_in: float32 [8, 1536, 2048], P('own', None, 'dp')
- grad_w_out: float32 [8, 2048, 1536], P('own', 'dp')
Inputs may be any that keep to these rules, and one draw needn't show every extreme that they name: `assign`: the two entries of a block name different experts. Among the 8 blocks of one index of dp no expert is named more than 5 times, and in every draw some expert is named exactly 5 times by the blocks of some index of dp.
All inputs are finite; a program needn't handle non-finite values.
Results may differ from a plain program's by a relative error of at most 0.012.
Values may be sent and summed in bfloat16 or wider, within the bound.
No kernel may reach another device: no remote copies, remote signals or barrier semaphores. Data moves between devices by JAX's collectives and lax.ppermute only.
A program may use at most 128 MiB of HBM per device.

v0:
```python
import functools

import jax
import jax.numpy as jnp
from jax import lax
from jax.experimental import pallas as pl
from jax.experimental.pallas import tpu as pltpu
from jax.sharding import Mesh, PartitionSpec as P


CAP = 5
BF = jnp.bfloat16
F32 = jnp.float32
OWN = ("y_lo", "x")
DP = ("y_hi", "z", "core")


def shift(value, axis, size, step):
    return lax.ppermute(value, axis, [(i, (i + step) % size) for i in range(size)])


def ring_up(value, ring):
    return shift(value, ring[0], 4, 1)


def ring_down(value, ring):
    return shift(value, ring[0], 4, 3)


def side_swap(value, ring):
    return shift(value, ring[1], 2, 1)


def core_swap(value):
    return shift(value, "core", 2, 1)


def y_step_down(value):
    at = [(y % 2) * 2 + y // 2 for y in range(4)]
    return lax.ppermute(value, ("y_lo", "y_hi"), [(at[y], at[(y + 3) % 4]) for y in range(4)])


def ring_gather(block, other, ring):
    below, above = ring_up(block, ring), ring_down(block, ring)
    other_below, other_above = ring_up(other, ring), ring_down(other, ring)
    far, other_far = ring_up(below, ring), ring_down(other_above, ring)
    return [block, other, below, other_below, above, other_above, far, other_far]


def plus(term, got):
    return (term.astype(F32) + got.astype(F32)).astype(BF)


def ring_scatter(near, down, up, far, ring):
    got_up = ring_up(far[0].astype(BF), ring)
    got_down = ring_down(far[1].astype(BF), ring)
    below_other = ring_up(up[1].astype(BF), ring)
    above_this = ring_down(down[0].astype(BF), ring)
    below_this = ring_up(plus(up[0], got_up), ring)
    above_other = ring_down(plus(down[1], got_down), ring)
    other = near[1].astype(F32) + below_other.astype(F32) + above_other.astype(F32)
    this = near[0].astype(F32) + below_this.astype(F32) + above_this.astype(F32)
    return this + side_swap(other.astype(BF), ring).astype(F32)


def gelu_cdf(values):
    return 0.5 * (1.0 + lax.erf(values * 0.7071067811865476))


def gelu_slope(values):
    return gelu_cdf(values) + values * jnp.exp(-0.5 * values * values) * 0.3989422804014327


def dot(a, b, dims):
    return lax.dot_general(a, b, (dims, ((), ())), preferred_element_type=F32)


def pick_kernel(blocks_ref, owners_ref, cot_ref, weight_ref, out_ref, whole_ref):
    part, block_len = cot_ref.shape[0] // 8, weight_ref.shape[1]

    def one(slot, carry):
        source = pl.ds(pl.multiple_of(blocks_ref[slot] * block_len, block_len), block_len)
        for position in range(8):
            at = pl.multiple_of(owners_ref[position] * part, part)
            whole_ref[pl.ds(at, part), :] = cot_ref[pl.ds(position * part, part), source]
        target = pl.ds(pl.multiple_of(slot * block_len, block_len), block_len)
        out_ref[target, :] = (whole_ref[...].T.astype(F32) * weight_ref[slot]).astype(BF)
        return carry

    lax.fori_loop(0, weight_ref.shape[0], one, 0)


def pick_rows(cot_t, blocks, owners, slot_weight):
    width = cot_t.shape[0]
    cap, block_len, _ = slot_weight.shape
    scalars, whole = pl.BlockSpec(memory_space=pltpu.SMEM), pl.BlockSpec(memory_space=pltpu.VMEM)
    return pl.pallas_call(
        pick_kernel,
        out_shape=jax.ShapeDtypeStruct((cap * block_len, width), BF),
        in_specs=[scalars, scalars, whole, whole],
        out_specs=whole,
        scratch_shapes=[pltpu.VMEM((width, block_len), BF)],
        compiler_params=pltpu.CompilerParams(vmem_limit_bytes=16 * 1024 * 1024),
        cost_estimate=pl.CostEstimate(flops=2000000, bytes_accessed=8000000, transcendentals=0),
    )(blocks, owners, cot_t, slot_weight)


def place_kernel(slots_ref, owners_ref, mine_ref, theirs_ref, weight_ref, out_ref):
    part, block_len = out_ref.shape[0] // 8, weight_ref.shape[2]

    def one(block, carry):
        source = pl.ds(pl.multiple_of(slots_ref[block] * block_len, block_len), block_len)
        target = pl.ds(pl.multiple_of(block * block_len, block_len), block_len)
        weight = weight_ref[block]
        for position in range(8):
            at = pl.ds(pl.multiple_of(owners_ref[position] * part, part), part)
            total = mine_ref[at, source].astype(F32) + theirs_ref[at, source].astype(F32)
            out_ref[pl.ds(position * part, part), target] = (total * weight).astype(BF)
        return carry

    lax.fori_loop(0, weight_ref.shape[0], one, 0)


def place_rows(mine, theirs, slots, owners, block_weight):
    count, _, block_len = block_weight.shape
    scalars, whole = pl.BlockSpec(memory_space=pltpu.SMEM), pl.BlockSpec(memory_space=pltpu.VMEM)
    return pl.pallas_call(
        place_kernel,
        out_shape=jax.ShapeDtypeStruct((theirs.shape[0], count * block_len), BF),
        in_specs=[scalars, scalars, whole, whole, whole],
        out_specs=whole,
        compiler_params=pltpu.CompilerParams(vmem_limit_bytes=24 * 1024 * 1024),
        cost_estimate=pl.CostEstimate(flops=3000000, bytes_accessed=9000000, transcendentals=0),
    )(slots, owners, mine, theirs, block_weight)


def join_kernel(axis, *refs):
    pieces, out_ref = refs[:-1], refs[-1]
    size = pieces[0].shape[axis]
    for place, piece in enumerate(pieces):
        at = pl.ds(place * size, size)
        if axis == 0:
            out_ref[at, :] = piece[...]
        else:
            out_ref[:, at] = piece[...]


def join(pieces, axis):
    shape = list(pieces[0].shape)
    shape[axis] *= len(pieces)
    whole = pl.BlockSpec(memory_space=pltpu.VMEM)
    return pl.pallas_call(
        functools.partial(join_kernel, axis),
        out_shape=jax.ShapeDtypeStruct(tuple(shape), BF),
        in_specs=[whole] * len(pieces),
        out_specs=whole,
        compiler_params=pltpu.CompilerParams(vmem_limit_bytes=16 * 1024 * 1024),
        cost_estimate=pl.CostEstimate(flops=0, bytes_accessed=6500000, transcendentals=0),
    )(*pieces)


Z_RING = ("z", "y_hi")


def body(tokens, assign, gates, cot, w_in, w_out):
    w_in, w_out = w_in[0], w_out[0]
    width, units = w_in.shape
    count = assign.shape[0]
    block_len = tokens.shape[0] // count
    expert = lax.axis_index(OWN).astype(jnp.int32)

    part = cot.shape[1]
    y_at = lax.axis_index("y_lo").astype(jnp.int32)
    position = jnp.arange(8, dtype=jnp.int32)
    owners = ((y_at + position) % 2) * 4 + position // 2

    in_blocks = ring_gather(w_in, side_swap(w_in, Z_RING), Z_RING)
    cot_other = side_swap(cot.T, ("x", "y_lo"))
    cot_side = jnp.concatenate([cot.T, cot_other], 0)
    cot_t = lax.all_gather(cot_side, "x", axis=0, tiled=True)

    is_first, is_second = assign[:, 0] == expert, assign[:, 1] == expert
    hit = jnp.logical_or(is_first, is_second)
    order = jnp.arange(count, dtype=jnp.int32)
    earlier = jnp.logical_and(order[None, :] < order[:, None], hit[None, :])
    rank = jnp.sum(earlier.astype(jnp.int32), axis=1)
    slots = jnp.minimum(rank, CAP - 1)
    slot_ids = jnp.arange(CAP, dtype=jnp.int32)
    match = jnp.logical_and(hit[None, :], rank[None, :] == slot_ids[:, None])
    blocks = jnp.sum(jnp.where(match, order[None, :], 0), axis=1)
    gate_blocks = gates.reshape(count, block_len, 2)
    block_weight = jnp.where(is_first[:, None], gate_blocks[..., 0], 0.0) + jnp.where(
        is_second[:, None], gate_blocks[..., 1], 0.0
    )
    slot_weight = jnp.sum(jnp.where(match[:, :, None], block_weight[None], 0.0), axis=1)
    hit_weight = jnp.broadcast_to(hit.astype(F32)[:, None], (count, block_len))

    half = CAP * block_len
    picked = tokens.reshape(count, block_len, width)[blocks].reshape(half, width)
    rows_other = core_swap(picked)
    rows = lax.optimization_barrier(jnp.concatenate([picked, rows_other], 0))
    full_in = join(in_blocks, 1)
    pre = dot(rows, full_in, ((1,), (0,)))
    act, act_slope = (pre * gelu_cdf(pre)).astype(BF), gelu_slope(pre).astype(BF)
    hidden, slope = lax.optimization_barrier((act, act_slope))

    out_other = y_step_down(y_step_down(w_out))
    out_blocks = ring_gather(w_out, out_other, Z_RING)
    grad_mine = pick_rows(cot_t, blocks, owners, slot_weight[..., None])
    grad_out = lax.optimization_barrier(jnp.concatenate([grad_mine, core_swap(grad_mine)], 0))

    group = 2 * units

    def four(terms_of):
        far = terms_of(3 * group, 4 * group)
        most = terms_of(0, 3 * group)
        return [(most[k], most[k + 1]) for k in (0, 2, 4)] + [(far[0], far[1])]

    def out_terms(start, stop):
        both = dot(hidden[:, start:stop], grad_out, ((0,), (0,))).astype(BF)
        return [both[k : k + units] for k in range(0, stop - start, units)]

    grad_w_out = ring_scatter(*four(out_terms), Z_RING)

    full_out = join(out_blocks, 0)

    def placed(value, matrix, dims, weight):
        both = dot(matrix, value, dims).astype(BF)
        theirs = core_swap(both[:, half:])
        parts = place_rows(both, theirs, slots, owners, weight[:, None])
        summed = lax.psum_scatter(parts, "x", scatter_dimension=0, tiled=True)
        other = side_swap(summed[part:], ("x", "y_lo"))
        return plus(summed[:part], other).T

    mixed = placed(hidden, full_out, ((0,), (1,)), block_weight)

    grad_hidden = dot(grad_out, full_out, ((1,), (1,)))
    grad_pre = (grad_hidden * slope.astype(F32)).astype(BF)
    grad_tokens = placed(grad_pre, full_in, ((1,), (1,)), hit_weight)

    def in_terms(start, stop):
        both = dot(rows, grad_pre[:, start:stop], ((0,), (0,))).astype(BF)
        return [both[:, k : k + units] for k in range(0, stop - start, units)]

    grad_w_in = ring_scatter(*four(in_terms), Z_RING)
    return mixed, grad_tokens, grad_w_in[None], grad_w_out[None]


def solution(mesh):
    split = Mesh(mesh.devices.reshape(2, 4, 2, 4, 2), OWN + DP)
    return jax.shard_map(
        body,
        mesh=split,
        in_specs=(
            P(DP, None),
            P(DP, None),
            P(DP, None),
            P(DP, OWN),
            P(OWN, None, DP),
            P(OWN, DP, None),
        ),
        out_specs=(P(DP, OWN), P(DP, OWN), P(OWN, None, DP), P(OWN, DP, None)),
        check_vma=False,
    )
```

profile of v0, /device:TPU:0, one launch (start us, length us, event | category | flops | bytes accessed | tf_op | source)
XLA Modules:
  0.0 230.1 jit_solution(5725740100753941471)
XLA Ops:
  9.5 2.1 gather_fusion
  11.5 3.3 %collective-permute-start.9 = (bf16[1536,128]{1,0:T(8,128)(2,1)S(1)}, bf16[1536,128]{1,0:T(8,128)(2,1)S(1)}, u32[]{:S(2)}, u32[]{:S(2)}) collective-permute-start(bf16[1536,128]{1,0:T(8,128)(2,1)S(1)} %bitcast.56), channel_id=1, source_target_pairs={{0,8},{8,0},{1,9},{9,1},{2,10},{10,2},{3,11},{11,3},{4,12},{12,4},... | collective-permute-start | bytes 1179656 | tf_op jit(solution)/shard_map/ppermute | solution.py:19
  14.8 1.9 collective-permute-start.10
  16.8 2.1 collective-permute-start.12
  19.9 4.7 %collective-permute-done.9.refs_1_ = bf16[1536,128]{1,0:T(8,128)(2,1)S(1)} collective-permute-done((bf16[1536,128]{1,0:T(8,128)(2,1)S(1)}, bf16[1536,128]{1,0:T(8,128)(2,1)S(1)}, u32[]{:S(2)}, u32[]{:S(2)}) %collective-permute-start.9) | collective-permute-done | bytes 393248 | tf_op jit(solution)/shard_map/ppermute | solution.py:19
  24.6 2.1 collective-permute-start.18
  28.7 2.9 %collective-permute-start.13 = (bf16[1536,128]{1,0:T(8,128)(2,1)S(1)}, bf16[1536,128]{1,0:T(8,128)(2,1)S(1)}, u32[]{:S(2)}, u32[]{:S(2)}) collective-permute-start(bf16[1536,128]{1,0:T(8,128)(2,1)S(1)} %collective-permute-done.9.refs_1_), channel_id=1, source_target_pairs={{0,6},{2,0},{4,2},{6,4},{1,7},{3,1},{5,3},{7,5},{8,14},{10,8},{12,... | collective-permute-start | bytes 1179656 | tf_op jit(solution)/shard_map/ppermute | solution.py:19
  31.6 2.3 %collective-permute-done = bf16[128,1536]{1,0:T(8,128)(2,1)S(1)} collective-permute-done((bf16[128,1536]{1,0:T(8,128)(2,1)}, bf16[128,1536]{1,0:T(8,128)(2,1)S(1)}, u32[]{:S(2)}, u32[]{:S(2)}) %collective-permute-start) | collective-permute-done | bytes 393248 | tf_op jit(solution)/shard_map/ppermute | solution.py:40
  33.9 2.2 collective-permute-start.1
  36.1 6.3 %collective-permute-done.18 = bf16[192,1024]{1,0:T(8,128)(2,1)S(1)} collective-permute-done((bf16[192,1024]{1,0:T(8,128)(2,1)}, bf16[192,1024]{1,0:T(8,128)(2,1)S(1)}, u32[]{:S(2)}, u32[]{:S(2)}) %collective-permute-start.18) | collective-permute-done | bytes 393248 | tf_op jit(solution)/shard_map/ppermute | solution.py:19
  42.4 1.9 collective-permute-start.11
  44.3 1.9 collective-permute-start.14
  47.5 2.9 %collective-permute-done.1.refs_1_ = bf16[128,1536]{1,0:T(8,128)(2,1)} collective-permute-done((bf16[128,1536]{1,0:T(8,128)(2,1)S(1)}, bf16[128,1536]{1,0:T(8,128)(2,1)}, u32[]{:S(2)}, u32[]{:S(2)}) %collective-permute-start.1) | collective-permute-done | bytes 393248 | tf_op jit(solution)/shard_map/ppermute | solution.py:40
  50.4 4.0 %collective-permute-start.5 = (bf16[128,1536]{1,0:T(8,128)(2,1)}, bf16[128,1536]{1,0:T(8,128)(2,1)}, u32[]{:S(2)}, u32[]{:S(2)}) collective-permute-start(bf16[128,1536]{1,0:T(8,128)(2,1)} %collective-permute-done.1.refs_1_), channel_id=1, source_target_pairs={{0,6},{2,0},{4,2},{6,4},{1,7},{3,1},{5,3},{7,5},{8,14},{10,8},{12,... | collective-permute-start | bytes 1179656 | tf_op jit(solution)/shard_map/ppermute | solution.py:19
  54.5 1.9 pad_maximum_fusion.2
  57.2 1.9 collective-permute-start.4
  59.1 4.2 %collective-permute-done.14.refs_6_ = bf16[1536,128]{1,0:T(8,128)(2,1)S(1)} collective-permute-done((bf16[1536,128]{1,0:T(8,128)(2,1)S(1)}, bf16[1536,128]{1,0:T(8,128)(2,1)S(1)}, u32[]{:S(2)}, u32[]{:S(2)}) %collective-permute-start.14) | collective-permute-done | bytes 393248 | tf_op jit(solution)/shard_map/ppermute | solution.py:19
  77.5 6.1 %collective-permute-done.3.refs_3_ = bf16[128,1536]{1,0:T(8,128)(2,1)S(1)} collective-permute-done((bf16[128,1536]{1,0:T(8,128)(2,1)}, bf16[128,1536]{1,0:T(8,128)(2,1)S(1)}, u32[]{:S(2)}, u32[]{:S(2)}) %collective-permute-start.3) | collective-permute-done | bytes 393248 | tf_op jit(solution)/shard_map/ppermute | solution.py:19
  85.0 2.9 %pad_maximum_fusion = bf16[1280,1536]{1,0:T(8,128)(2,1)S(1)} fusion(bf16[640,1536]{1,0:T(8,128)(2,1)} %collective-permute-done.8, bf16[640,1536]{1,0:T(8,128)(2,1)S(1)} %bitcast.65), kind=kLoop, calls=%fused_computation.12 | loop fusion | flops 7864320 | bytes 7864320 | tf_op jit(solution)/shard_map/concatenate | solution.py:201
  88.0 7.1 %fusion.4 = (bf16[1280,1024]{1,0:T(8,128)(2,1)}, bf16[1280,1024]{1,0:T(8,128)(2,1)S(1)}) fusion(bf16[1280,1536]{1,0:T(8,128)(2,1)S(1)} %pad_maximum_fusion, bf16[1536,1024]{1,0:T(8,128)(2,1)S(1)} %shard_map.94), kind=kOutput, calls=%fused_computation.8 | convolution fusion | flops 4040949760 | bytes 12320768 | tf_op jit(solution)/shard_map/dot_general | solution.py:75
  96.7 4.6 %convolution_convert_fusion.1.mine_ref = bf16[1536,1280]{1,0:T(8,128)(2,1)S(1)} fusion(bf16[1024,1536]{1,0:T(8,128)(2,1)S(1)} %shard_map.93, bf16[1280,1024]{1,0:T(8,128)(2,1)S(1)} %get-tuple-element.6), kind=kOutput, calls=%fused_computation.3 | convolution fusion | flops 4028497920 | bytes 9699328 | tf_op jit(solution)/shard_map/dot_general | solution.py:75
  102.7 1.9 copy-done.2
  105.1 1.9 copy-done.6
  107.0 2.2 shard_map.96
  109.9 4.3 %shard_map.95 = bf16[1536,1024]{1,0:T(8,128)(2,1)} custom-call(s32[8]{0:T(128)S(1)} %broadcast_minimum_fusion.slots_ref, s32[8]{0:T(128)S(1)} %fusion.15.owners_ref, bf16[1536,1280]{1,0:T(8,128)(2,1)S(1)} %copy-done.3, bf16[1536,640]{1,0:T(8,128)(2,1)} %collective-permute-done.16.theirs_ref, f32[8,1,128]{2,1,0:T(1,128)S(1)} %fusion.11.weight_ref), custom_call_target="tpu_custom_call" | custom-call | flops 3000000 | bytes 9000000 | tf_op jit(solution)/shard_map/pallas_call | solution.py:127
  114.3 2.0 pad_maximum_fusion.1
  117.6 4.6 %multiply_convert_fusion = bf16[1280,1024]{1,0:T(8,128)(2,1)S(1)} fusion(bf16[1280,1024]{1,0:T(8,128)(2,1)S(1)} %copy-done.41, bf16[1280,1536]{1,0:T(8,128)(2,1)S(1)} %pad_maximum_fusion.1, bf16[1024,1536]{1,0:T(8,128)(2,1)S(1)} %copy-done.8), kind=kOutput, calls=%fused_computation.9 | convolution fusion | flops 4030464000 | bytes 12320768 | tf_op jit(solution)/shard_map/dot_general | solution.py:75
  122.2 4.6 %convolution_convert_fusion.mine_ref = bf16[1536,1280]{1,0:T(8,128)(2,1)S(1)} fusion(bf16[1536,1024]{1,0:T(8,128)(2,1)S(1)} %copy-done.5, bf16[1280,1024]{1,0:T(8,128)(2,1)S(1)} %multiply_convert_fusion), kind=kOutput, calls=%fused_computation.2 | convolution fusion | flops 4028497920 | bytes 9699328 | tf_op jit(solution)/shard_map/dot_general | solution.py:75
  127.1 2.3 convolution_convert_fusion.4
  131.1 3.3 %shard_map.97 = bf16[1536,1024]{1,0:T(8,128)(2,1)} custom-call(s32[8]{0:T(128)S(1)} %broadcast_minimum_fusion.slots_ref, s32[8]{0:T(128)S(1)} %fusion.15.owners_ref, bf16[1536,1280]{1,0:T(8,128)(2,1)S(1)} %convolution_convert_fusion.mine_ref, bf16[1536,640]{1,0:T(8,128)(2,1)S(1)} %collective-permute-done.20.theirs_ref, ...), custom_call_target="tpu_custom_call" | custom-call | flops 3000000 | bytes 9000000 | tf_op jit(solution)/shard_map/pallas_call | solution.py:127
  134.6 3.2 %collective-permute-start.33 = (bf16[128,1536]{1,0:T(8,128)(2,1)S(1)}, bf16[128,1536]{1,0:T(8,128)(2,1)S(1)}, u32[]{:S(2)}, u32[]{:S(2)}) collective-permute-start(bf16[128,1536]{1,0:T(8,128)(2,1)S(1)} %get-tuple-element.21), channel_id=1, source_target_pairs={{0,6},{2,0},{4,2},{6,4},{1,7},{3,1},{5,3},{7,5},{8,14},{10,8},{12,... | collective-permute-start | bytes 1179656 | tf_op jit(solution)/shard_map/ppermute | solution.py:19
  137.8 6.0 %convolution_convert_fusion.2 = bf16[768,1536]{1,0:T(8,128)(2,1)S(1)} fusion(bf16[1280,1536]{1,0:T(8,128)(2,1)} %copy-done.28, bf16[1280,1024]{1,0:T(8,128)(2,1)} %copy-done.38), kind=kOutput, calls=%fused_computation.14 | convolution fusion | flops 3021078528 | bytes 8257536 | tf_op jit(solution)/shard_map/dot_general | solution.py:75
  144.0 3.2 %collective-permute-start.31 = (bf16[128,1536]{1,0:T(8,128)(2,1)S(1)}, bf16[128,1536]{1,0:T(8,128)(2,1)S(1)}, u32[]{:S(2)}, u32[]{:S(2)}) collective-permute-start(bf16[128,1536]{1,0:T(8,128)(2,1)S(1)} %get-tuple-element.14), channel_id=1, source_target_pairs={{0,6},{2,0},{4,2},{6,4},{1,7},{3,1},{5,3},{7,5},{8,14},{10,8},{12,... | collective-permute-start | bytes 1179656 | tf_op jit(solution)/shard_map/ppermute | solution.py:19
  148.8 3.6 %convolution_convert_fusion.3 = bf16[1536,768]{1,0:T(8,128)(2,1)S(1)} fusion(bf16[1280,1536]{1,0:T(8,128)(2,1)S(1)} %copy-done.27, bf16[1280,1024]{1,0:T(8,128)(2,1)S(1)} %copy-done.40), kind=kOutput, calls=%fused_computation.15 | convolution fusion | flops 3021078528 | bytes 8257536 | tf_op jit(solution)/shard_map/dot_general | solution.py:75
  153.3 3.2 %collective-permute-start.26 = (bf16[1536,128]{1,0:T(8,128)(2,1)S(1)}, bf16[1536,128]{1,0:T(8,128)(2,1)S(1)}, u32[]{:S(2)}, u32[]{:S(2)}) collective-permute-start(bf16[1536,128]{1,0:T(8,128)(2,1)S(1)} %get-tuple-element.23), channel_id=1, source_target_pairs={{0,6},{2,0},{4,2},{6,4},{1,7},{3,1},{5,3},{7,5},{8,14},{10,8},{12,... | collective-permute-start | bytes 1179656 | tf_op jit(solution)/shard_map/ppermute | solution.py:19
  156.7 8.9 %collective-permute-done.22 = bf16[1536,128]{1,0:T(8,128)(2,1)S(1)} collective-permute-done((bf16[1536,128]{1,0:T(8,128)(2,1)S(1)}, bf16[1536,128]{1,0:T(8,128)(2,1)S(1)}, u32[]{:S(2)}, u32[]{:S(2)}) %collective-permute-start.22) | collective-permute-done | bytes 393248 | tf_op jit(solution)/shard_map/ppermute | solution.py:19
  165.6 2.2 collective-permute-start.34
  168.7 14.7 %collective-permute-done.34 = bf16[128,1536]{1,0:T(8,128)(2,1)S(1)} collective-permute-done((bf16[128,1536]{1,0:T(8,128)(2,1)S(1)}, bf16[128,1536]{1,0:T(8,128)(2,1)S(1)}, u32[]{:S(2)}, u32[]{:S(2)}) %collective-permute-start.34) | collective-permute-done | bytes 393248 | tf_op jit(solution)/shard_map/ppermute | solution.py:19
  185.6 5.5 %collective-permute-done.27 = bf16[1536,128]{1,0:T(8,128)(2,1)S(1)} collective-permute-done((bf16[1536,128]{1,0:T(8,128)(2,1)S(1)}, bf16[1536,128]{1,0:T(8,128)(2,1)S(1)}, u32[]{:S(2)}, u32[]{:S(2)}) %collective-permute-start.27) | collective-permute-done | bytes 393248 | tf_op jit(solution)/shard_map/ppermute | solution.py:19
  191.2 1.8 collective-permute-start.35
  195.6 9.0 %collective-permute-done.35 = bf16[128,1536]{1,0:T(8,128)(2,1)S(1)} collective-permute-done((bf16[128,1536]{1,0:T(8,128)(2,1)S(1)}, bf16[128,1536]{1,0:T(8,128)(2,1)S(1)}, u32[]{:S(2)}, u32[]{:S(2)}) %collective-permute-start.35) | collective-permute-done | bytes 393248 | tf_op jit(solution)/shard_map/ppermute | solution.py:19
  205.7 1.9 slice.126
  208.8 2.1 collective-permute-start.21
  210.9 2.3 collective-permute-done.28
  213.2 2.3 add_bitcast_fusion.1
  215.5 3.1 %collective-permute-done.17 = bf16[192,1024]{1,0:T(8,128)(2,1)} collective-permute-done((bf16[192,1024]{1,0:T(8,128)(2,1)}, bf16[192,1024]{1,0:T(8,128)(2,1)}, u32[]{:S(2)}, u32[]{:S(2)}) %collective-permute-start.17) | collective-permute-done | bytes 393248 | tf_op jit(solution)/shard_map/ppermute | solution.py:19
  218.6 1.9 fusion.9
  220.4 2.2 collective-permute-done.21
  (165 shorter events, 42.3 us)
Async XLA Ops:
  7.2 97.9 %all-gather.2.cloned.1.call-start = ((), (), s32[]{:S(2)}) async-start(), calls=%async_computation.3 | async-start | bytes 3932160 | tf_op jit(solution)/shard_map/all_gather | solution.py:180
  11.5 73.5 %collective-permute-start.8 = (bf16[640,1536]{1,0:T(8,128)(2,1)}, bf16[640,1536]{1,0:T(8,128)(2,1)}, u32[]{:S(2)}, u32[]{:S(2)}) collective-permute-start(bf16[640,1536]{1,0:T(8,128)(2,1)} %bitcast.64), channel_id=1, source_target_pairs={{0,1},{1,0},{2,3},{3,2},{4,5},{5,4},{6,7},{7,6},{8,9},{9,8},{10,11... | collective-permute-start | bytes 5898248 | tf_op jit(solution)/shard_map/ppermute | solution.py:19
  11.5 13.1 %collective-permute-start.9 = (bf16[1536,128]{1,0:T(8,128)(2,1)S(1)}, bf16[1536,128]{1,0:T(8,128)(2,1)S(1)}, u32[]{:S(2)}, u32[]{:S(2)}) collective-permute-start(bf16[1536,128]{1,0:T(8,128)(2,1)S(1)} %bitcast.56), channel_id=1, source_target_pairs={{0,8},{8,0},{1,9},{9,1},{2,10},{10,2},{3,11},{11,3},{4,12},{12,4},... | collective-permute-start | bytes 1179656 | tf_op jit(solution)/shard_map/ppermute | solution.py:19
  14.8 13.5 %collective-permute-start.10 = (bf16[1536,128]{1,0:T(8,128)(2,1)S(1)}, bf16[1536,128]{1,0:T(8,128)(2,1)S(1)}, u32[]{:S(2)}, u32[]{:S(2)}) collective-permute-start(bf16[1536,128]{1,0:T(8,128)(2,1)S(1)} %bitcast.57), channel_id=1, source_target_pairs={{0,2},{2,4},{4,6},{6,0},{1,3},{3,5},{5,7},{7,1},{8,10},{10,12},{12... | collective-permute-start | bytes 1179656 | tf_op jit(solution)/shard_map/ppermute | solution.py:19
  16.8 11.9 %collective-permute-start.12 = (bf16[1536,128]{1,0:T(8,128)(2,1)S(1)}, bf16[1536,128]{1,0:T(8,128)(2,1)S(1)}, u32[]{:S(2)}, u32[]{:S(2)}) collective-permute-start(bf16[1536,128]{1,0:T(8,128)(2,1)S(1)} %bitcast.58), channel_id=1, source_target_pairs={{0,6},{2,0},{4,2},{6,4},{1,7},{3,1},{5,3},{7,5},{8,14},{10,8},{12,... | collective-permute-start | bytes 1179656 | tf_op jit(solution)/shard_map/ppermute | solution.py:19
  18.9 15.1 %collective-permute-start = (bf16[128,1536]{1,0:T(8,128)(2,1)}, bf16[128,1536]{1,0:T(8,128)(2,1)S(1)}, u32[]{:S(2)}, u32[]{:S(2)}) collective-permute-start(bf16[128,1536]{1,0:T(8,128)(2,1)} %bitcast.60), channel_id=1, source_target_pairs={{0,72},{64,0},{8,64},{72,8},{1,73},{65,1},{9,65},{73,9},{2,74},{66... | collective-permute-start | bytes 1179656 | tf_op jit(solution)/shard_map/ppermute | solution.py:40
  24.6 42.1 %copy-start.11 = (bf16[1536,128]{1,0:T(8,128)(2,1)}, bf16[1536,128]{1,0:T(8,128)(2,1)S(1)}, u32[]{:S(2)}) copy-start(bf16[1536,128]{1,0:T(8,128)(2,1)S(1)} %collective-permute-done.9.refs_1_) | copy-start | bytes 1179652
  24.6 17.7 %collective-permute-start.18 = (bf16[192,1024]{1,0:T(8,128)(2,1)}, bf16[192,1024]{1,0:T(8,128)(2,1)S(1)}, u32[]{:S(2)}, u32[]{:S(2)}) collective-permute-start(bf16[192,1024]{1,0:T(8,128)(2,1)} %bitcast.66), channel_id=1, source_target_pairs={{0,64},{64,0},{1,65},{65,1},{2,66},{66,2},{3,67},{67,3},{4,68},{68... | collective-permute-start | bytes 1179656 | tf_op jit(solution)/shard_map/ppermute | solution.py:19
  28.4 38.4 %copy-start.13 = (bf16[1536,128]{1,0:T(8,128)(2,1)}, bf16[1536,128]{1,0:T(8,128)(2,1)S(1)}, u32[]{:S(2)}) copy-start(bf16[1536,128]{1,0:T(8,128)(2,1)S(1)} %collective-permute-done.10.refs_2_) | copy-start | bytes 1179652
  28.4 15.9 %collective-permute-start.2 = (bf16[128,1536]{1,0:T(8,128)(2,1)}, bf16[128,1536]{1,0:T(8,128)(2,1)}, u32[]{:S(2)}, u32[]{:S(2)}) collective-permute-start(bf16[128,1536]{1,0:T(8,128)(2,1)} %bitcast.61), channel_id=1, source_target_pairs={{0,2},{2,4},{4,6},{6,0},{1,3},{3,5},{5,7},{7,1},{8,10},{10,12},{12... | collective-permute-start | bytes 1179656 | tf_op jit(solution)/shard_map/ppermute | solution.py:19
  28.7 38.1 %copy-start.15 = (bf16[1536,128]{1,0:T(8,128)(2,1)}, bf16[1536,128]{1,0:T(8,128)(2,1)S(1)}, u32[]{:S(2)}) copy-start(bf16[1536,128]{1,0:T(8,128)(2,1)S(1)} %collective-permute-done.12.refs_4_) | copy-start | bytes 1179652
  28.7 17.5 %collective-permute-start.13 = (bf16[1536,128]{1,0:T(8,128)(2,1)S(1)}, bf16[1536,128]{1,0:T(8,128)(2,1)S(1)}, u32[]{:S(2)}, u32[]{:S(2)}) collective-permute-start(bf16[1536,128]{1,0:T(8,128)(2,1)S(1)} %collective-permute-done.9.refs_1_), channel_id=1, source_target_pairs={{0,6},{2,0},{4,2},{6,4},{1,7},{3,1},{5,3},{7,5},{8,14},{10,8},{12,... | collective-permute-start | bytes 1179656 | tf_op jit(solution)/shard_map/ppermute | solution.py:19
  33.9 16.5 %collective-permute-start.1 = (bf16[128,1536]{1,0:T(8,128)(2,1)S(1)}, bf16[128,1536]{1,0:T(8,128)(2,1)}, u32[]{:S(2)}, u32[]{:S(2)}) collective-permute-start(bf16[128,1536]{1,0:T(8,128)(2,1)S(1)} %collective-permute-done), channel_id=1, source_target_pairs={{0,72},{64,0},{8,64},{72,8},{1,73},{65,1},{9,65},{73,9},{2,74},{66... | collective-permute-start | bytes 1179656 | tf_op jit(solution)/shard_map/ppermute | solution.py:40
  42.4 14.1 %collective-permute-start.11 = (bf16[1536,128]{1,0:T(8,128)(2,1)S(1)}, bf16[1536,128]{1,0:T(8,128)(2,1)S(1)}, u32[]{:S(2)}, u32[]{:S(2)}) collective-permute-start(bf16[1536,128]{1,0:T(8,128)(2,1)S(1)} %collective-permute-done.9.refs_1_), channel_id=1, source_target_pairs={{0,2},{2,4},{4,6},{6,0},{1,3},{3,5},{5,7},{7,1},{8,10},{10,12},{12... | collective-permute-start | bytes 1179656 | tf_op jit(solution)/shard_map/ppermute | solution.py:19
  44.3 19.0 %collective-permute-start.14 = (bf16[1536,128]{1,0:T(8,128)(2,1)S(1)}, bf16[1536,128]{1,0:T(8,128)(2,1)S(1)}, u32[]{:S(2)}, u32[]{:S(2)}) collective-permute-start(bf16[1536,128]{1,0:T(8,128)(2,1)S(1)} %collective-permute-done.10.refs_2_), channel_id=1, source_target_pairs={{0,2},{2,4},{4,6},{6,0},{1,3},{3,5},{5,7},{7,1},{8,10},{10,12},{12... | collective-permute-start | bytes 1179656 | tf_op jit(solution)/shard_map/ppermute | solution.py:19
  46.2 20.5 %copy-start.17 = (bf16[1536,128]{1,0:T(8,128)(2,1)}, bf16[1536,128]{1,0:T(8,128)(2,1)S(1)}, u32[]{:S(2)}) copy-start(bf16[1536,128]{1,0:T(8,128)(2,1)S(1)} %collective-permute-done.13.refs_5_) | copy-start | bytes 1179652
  46.2 17.8 %collective-permute-start.15 = (bf16[1536,128]{1,0:T(8,128)(2,1)S(1)}, bf16[1536,128]{1,0:T(8,128)(2,1)S(1)}, u32[]{:S(2)}, u32[]{:S(2)}) collective-permute-start(bf16[1536,128]{1,0:T(8,128)(2,1)S(1)} %collective-permute-done.13.refs_5_), channel_id=1, source_target_pairs={{0,6},{2,0},{4,2},{6,4},{1,7},{3,1},{5,3},{7,5},{8,14},{10,8},{12,... | collective-permute-start | bytes 1179656 | tf_op jit(solution)/shard_map/ppermute | solution.py:19
  50.4 16.3 %collective-permute-start.5 = (bf16[128,1536]{1,0:T(8,128)(2,1)}, bf16[128,1536]{1,0:T(8,128)(2,1)}, u32[]{:S(2)}, u32[]{:S(2)}) collective-permute-start(bf16[128,1536]{1,0:T(8,128)(2,1)} %collective-permute-done.1.refs_1_), channel_id=1, source_target_pairs={{0,6},{2,0},{4,2},{6,4},{1,7},{3,1},{5,3},{7,5},{8,14},{10,8},{12,... | collective-permute-start | bytes 1179656 | tf_op jit(solution)/shard_map/ppermute | solution.py:19
  56.4 149.3 %reduce-scatter.3.cloned.1.call-start = ((), (), s32[]{:S(2)}) async-start(), calls=%async_computation.2 | async-start | bytes 3932160 | tf_op jit(solution)/shard_map/reduce_scatter | solution.py:231
  56.5 27.1 %copy-start.10 = (bf16[1,128,1536]{2,1,0:T(8,128)(2,1)S(1)}, bf16[1,128,1536]{2,1,0:T(8,128)(2,1)}, u32[]{:S(2)}) copy-start(bf16[1,128,1536]{2,1,0:T(8,128)(2,1)} %param.11) | copy-start | bytes 1179652
  57.2 18.8 %collective-permute-start.4 = (bf16[128,1536]{1,0:T(8,128)(2,1)}, bf16[128,1536]{1,0:T(8,128)(2,1)S(1)}, u32[]{:S(2)}, u32[]{:S(2)}) collective-permute-start(bf16[128,1536]{1,0:T(8,128)(2,1)} %bitcast.62), channel_id=1, source_target_pairs={{0,6},{2,0},{4,2},{6,4},{1,7},{3,1},{5,3},{7,5},{8,14},{10,8},{12,... | collective-permute-start | bytes 1179656 | tf_op jit(solution)/shard_map/ppermute | solution.py:19
  64.0 13.4 %collective-permute-start.6 = (bf16[128,1536]{1,0:T(8,128)(2,1)}, bf16[128,1536]{1,0:T(8,128)(2,1)S(1)}, u32[]{:S(2)}, u32[]{:S(2)}) collective-permute-start(bf16[128,1536]{1,0:T(8,128)(2,1)} %collective-permute-done.2.refs_2_), channel_id=1, source_target_pairs={{0,2},{2,4},{4,6},{6,0},{1,3},{3,5},{5,7},{7,1},{8,10},{10,12},{12... | collective-permute-start | bytes 1179656 | tf_op jit(solution)/shard_map/ppermute | solution.py:19
  64.8 18.7 %collective-permute-start.3 = (bf16[128,1536]{1,0:T(8,128)(2,1)}, bf16[128,1536]{1,0:T(8,128)(2,1)S(1)}, u32[]{:S(2)}, u32[]{:S(2)}) collective-permute-start(bf16[128,1536]{1,0:T(8,128)(2,1)} %collective-permute-done.1.refs_1_), channel_id=1, source_target_pairs={{0,2},{2,4},{4,6},{6,0},{1,3},{3,5},{5,7},{7,1},{8,10},{10,12},{12... | collective-permute-start | bytes 1179656 | tf_op jit(solution)/shard_map/ppermute | solution.py:19
  66.8 16.8 %collective-permute-start.7 = (bf16[128,1536]{1,0:T(8,128)(2,1)}, bf16[128,1536]{1,0:T(8,128)(2,1)S(1)}, u32[]{:S(2)}, u32[]{:S(2)}) collective-permute-start(bf16[128,1536]{1,0:T(8,128)(2,1)} %collective-permute-done.5.refs_5_), channel_id=1, source_target_pairs={{0,6},{2,0},{4,2},{6,4},{1,7},{3,1},{5,3},{7,5},{8,14},{10,8},{12,... | collective-permute-start | bytes 1179656 | tf_op jit(solution)/shard_map/ppermute | solution.py:19
  104.7 5.3 %collective-permute-start.16 = (bf16[1536,640]{1,0:T(8,128)(2,1)}, bf16[1536,640]{1,0:T(8,128)(2,1)}, u32[]{:S(2)}, u32[]{:S(2)}) collective-permute-start(bf16[1536,640]{1,0:T(8,128)(2,1)} %slice.122), channel_id=1, source_target_pairs={{0,1},{1,0},{2,3},{3,2},{4,5},{5,4},{6,7},{7,6},{8,9},{9,8},{10,11... | collective-permute-start | bytes 5898248 | tf_op jit(solution)/shard_map/ppermute | solution.py:19
  109.2 5.1 %collective-permute-start.19 = (bf16[640,1536]{1,0:T(8,128)(2,1)S(1)}, bf16[640,1536]{1,0:T(8,128)(2,1)}, u32[]{:S(2)}, u32[]{:S(2)}) collective-permute-start(bf16[640,1536]{1,0:T(8,128)(2,1)S(1)} %shard_map.96), channel_id=1, source_target_pairs={{0,1},{1,0},{2,3},{3,2},{4,5},{5,4},{6,7},{7,6},{8,9},{9,8},{10,11... | collective-permute-start | bytes 5898248 | tf_op jit(solution)/shard_map/ppermute | solution.py:19
  114.2 93.4 %reduce-scatter.5.cloned.1.call-start = ((), (), s32[]{:S(2)}) async-start(), calls=%async_computation.4 | async-start | bytes 3932160 | tf_op jit(solution)/shard_map/reduce_scatter | solution.py:231
  127.0 4.1 %collective-permute-start.20 = (bf16[1536,640]{1,0:T(8,128)(2,1)S(1)}, bf16[1536,640]{1,0:T(8,128)(2,1)S(1)}, u32[]{:S(2)}, u32[]{:S(2)}) collective-permute-start(bf16[1536,640]{1,0:T(8,128)(2,1)S(1)} %slice.127), channel_id=1, source_target_pairs={{0,1},{1,0},{2,3},{3,2},{4,5},{5,4},{6,7},{7,6},{8,9},{9,8},{10,11... | collective-permute-start | bytes 5898248 | tf_op jit(solution)/shard_map/ppermute | solution.py:19
  134.5 18.8 %collective-permute-start.29 = (bf16[128,1536]{1,0:T(8,128)(2,1)S(1)}, bf16[128,1536]{1,0:T(8,128)(2,1)S(1)}, u32[]{:S(2)}, u32[]{:S(2)}) collective-permute-start(bf16[128,1536]{1,0:T(8,128)(2,1)S(1)} %get-tuple-element.20), channel_id=1, source_target_pairs={{0,2},{2,4},{4,6},{6,0},{1,3},{3,5},{5,7},{7,1},{8,10},{10,12},{12... | collective-permute-start | bytes 1179656 | tf_op jit(solution)/shard_map/ppermute | solution.py:19
  134.6 12.6 %copy-start.27 = (bf16[1280,1536]{1,0:T(8,128)(2,1)S(1)}, bf16[1280,1536]{1,0:T(8,128)(2,1)}, u32[]{:S(2)}) copy-start(bf16[1280,1536]{1,0:T(8,128)(2,1)} %copy-done.26) | copy-start | bytes 11796484
  134.6 21.9 %collective-permute-start.33 = (bf16[128,1536]{1,0:T(8,128)(2,1)S(1)}, bf16[128,1536]{1,0:T(8,128)(2,1)S(1)}, u32[]{:S(2)}, u32[]{:S(2)}) collective-permute-start(bf16[128,1536]{1,0:T(8,128)(2,1)S(1)} %get-tuple-element.21), channel_id=1, source_target_pairs={{0,6},{2,0},{4,2},{6,4},{1,7},{3,1},{5,3},{7,5},{8,14},{10,8},{12,... | collective-permute-start | bytes 1179656 | tf_op jit(solution)/shard_map/ppermute | solution.py:19
  143.9 24.8 %collective-permute-start.32 = (bf16[128,1536]{1,0:T(8,128)(2,1)S(1)}, bf16[128,1536]{1,0:T(8,128)(2,1)S(1)}, u32[]{:S(2)}, u32[]{:S(2)}) collective-permute-start(bf16[128,1536]{1,0:T(8,128)(2,1)S(1)} %get-tuple-element.15), channel_id=1, source_target_pairs={{0,2},{2,4},{4,6},{6,0},{1,3},{3,5},{5,7},{7,1},{8,10},{10,12},{12... | collective-permute-start | bytes 1179656 | tf_op jit(solution)/shard_map/ppermute | solution.py:19
  144.0 50.0 %collective-permute-start.31 = (bf16[128,1536]{1,0:T(8,128)(2,1)S(1)}, bf16[128,1536]{1,0:T(8,128)(2,1)S(1)}, u32[]{:S(2)}, u32[]{:S(2)}) collective-permute-start(bf16[128,1536]{1,0:T(8,128)(2,1)S(1)} %get-tuple-element.14), channel_id=1, source_target_pairs={{0,6},{2,0},{4,2},{6,4},{1,7},{3,1},{5,3},{7,5},{8,14},{10,8},{12,... | collective-permute-start | bytes 1179656 | tf_op jit(solution)/shard_map/ppermute | solution.py:19
  148.5 17.1 %collective-permute-start.22 = (bf16[1536,128]{1,0:T(8,128)(2,1)S(1)}, bf16[1536,128]{1,0:T(8,128)(2,1)S(1)}, u32[]{:S(2)}, u32[]{:S(2)}) collective-permute-start(bf16[1536,128]{1,0:T(8,128)(2,1)S(1)} %get-tuple-element.22), channel_id=1, source_target_pairs={{0,2},{2,4},{4,6},{6,0},{1,3},{3,5},{5,7},{7,1},{8,10},{10,12},{12... | collective-permute-start | bytes 1179656 | tf_op jit(solution)/shard_map/ppermute | solution.py:19
  152.4 40.6 %copy-start.29 = (bf16[1536,768]{1,0:T(8,128)(2,1)}, bf16[1536,768]{1,0:T(8,128)(2,1)S(1)}, u32[]{:S(2)}) copy-start(bf16[1536,768]{1,0:T(8,128)(2,1)S(1)} %convolution_convert_fusion.3) | copy-start | bytes 7077892
  153.3 12.3 %collective-permute-start.26 = (bf16[1536,128]{1,0:T(8,128)(2,1)S(1)}, bf16[1536,128]{1,0:T(8,128)(2,1)S(1)}, u32[]{:S(2)}, u32[]{:S(2)}) collective-permute-start(bf16[1536,128]{1,0:T(8,128)(2,1)S(1)} %get-tuple-element.23), channel_id=1, source_target_pairs={{0,6},{2,0},{4,2},{6,4},{1,7},{3,1},{5,3},{7,5},{8,14},{10,8},{12,... | collective-permute-start | bytes 1179656 | tf_op jit(solution)/shard_map/ppermute | solution.py:19
  156.5 28.0 %collective-permute-start.25 = (bf16[1536,128]{1,0:T(8,128)(2,1)S(1)}, bf16[1536,128]{1,0:T(8,128)(2,1)S(1)}, u32[]{:S(2)}, u32[]{:S(2)}) collective-permute-start(bf16[1536,128]{1,0:T(8,128)(2,1)S(1)} %get-tuple-element.19), channel_id=1, source_target_pairs={{0,2},{2,4},{4,6},{6,0},{1,3},{3,5},{5,7},{7,1},{8,10},{10,12},{12... | collective-permute-start | bytes 1179656 | tf_op jit(solution)/shard_map/ppermute | solution.py:19
  165.6 45.3 %collective-permute-start.24 = (bf16[1536,128]{1,0:T(8,128)(2,1)}, bf16[1536,128]{1,0:T(8,128)(2,1)S(1)}, u32[]{:S(2)}, u32[]{:S(2)}) collective-permute-start(bf16[1536,128]{1,0:T(8,128)(2,1)} %get-tuple-element.18), channel_id=1, source_target_pairs={{0,6},{2,0},{4,2},{6,4},{1,7},{3,1},{5,3},{7,5},{8,14},{10,8},{12,... | collective-permute-start | bytes 1179656 | tf_op jit(solution)/shard_map/ppermute | solution.py:19
  165.6 17.8 %collective-permute-start.34 = (bf16[128,1536]{1,0:T(8,128)(2,1)S(1)}, bf16[128,1536]{1,0:T(8,128)(2,1)S(1)}, u32[]{:S(2)}, u32[]{:S(2)}) collective-permute-start(bf16[128,1536]{1,0:T(8,128)(2,1)S(1)} %get-tuple-element.13), channel_id=1, source_target_pairs={{0,6},{2,0},{4,2},{6,4},{1,7},{3,1},{5,3},{7,5},{8,14},{10,8},{12,... | collective-permute-start | bytes 1179656 | tf_op jit(solution)/shard_map/ppermute | solution.py:19
  168.7 26.9 %collective-permute-start.30 = (bf16[128,1536]{1,0:T(8,128)(2,1)S(1)}, bf16[128,1536]{1,0:T(8,128)(2,1)S(1)}, u32[]{:S(2)}, u32[]{:S(2)}) collective-permute-start(bf16[128,1536]{1,0:T(8,128)(2,1)S(1)} %get-tuple-element.12), channel_id=1, source_target_pairs={{0,2},{2,4},{4,6},{6,0},{1,3},{3,5},{5,7},{7,1},{8,10},{10,12},{12... | collective-permute-start | bytes 1179656 | tf_op jit(solution)/shard_map/ppermute | solution.py:19
  183.4 7.8 %collective-permute-start.27 = (bf16[1536,128]{1,0:T(8,128)(2,1)S(1)}, bf16[1536,128]{1,0:T(8,128)(2,1)S(1)}, u32[]{:S(2)}, u32[]{:S(2)}) collective-permute-start(bf16[1536,128]{1,0:T(8,128)(2,1)S(1)} %get-tuple-element.17), channel_id=1, source_target_pairs={{0,6},{2,0},{4,2},{6,4},{1,7},{3,1},{5,3},{7,5},{8,14},{10,8},{12,... | collective-permute-start | bytes 1179656 | tf_op jit(solution)/shard_map/ppermute | solution.py:19
  184.5 26.4 %collective-permute-start.23 = (bf16[1536,128]{1,0:T(8,128)(2,1)}, bf16[1536,128]{1,0:T(8,128)(2,1)}, u32[]{:S(2)}, u32[]{:S(2)}) collective-permute-start(bf16[1536,128]{1,0:T(8,128)(2,1)} %get-tuple-element.16), channel_id=1, source_target_pairs={{0,2},{2,4},{4,6},{6,0},{1,3},{3,5},{5,7},{7,1},{8,10},{10,12},{12... | collective-permute-start | bytes 1179656 | tf_op jit(solution)/shard_map/ppermute | solution.py:19
  191.2 13.5 %collective-permute-start.35 = (bf16[128,1536]{1,0:T(8,128)(2,1)S(1)}, bf16[128,1536]{1,0:T(8,128)(2,1)S(1)}, u32[]{:S(2)}, u32[]{:S(2)}) collective-permute-start(bf16[128,1536]{1,0:T(8,128)(2,1)S(1)} %add_convert_fusion), channel_id=1, source_target_pairs={{0,8},{8,0},{1,9},{9,1},{2,10},{10,2},{3,11},{11,3},{4,12},{12,4},... | collective-permute-start | bytes 1179656 | tf_op jit(solution)/shard_map/ppermute | solution.py:19
  193.9 19.3 %collective-permute-start.28 = (bf16[1536,128]{1,0:T(8,128)(2,1)}, bf16[1536,128]{1,0:T(8,128)(2,1)}, u32[]{:S(2)}, u32[]{:S(2)}) collective-permute-start(bf16[1536,128]{1,0:T(8,128)(2,1)} %add_convert_fusion.3), channel_id=1, source_target_pairs={{0,8},{8,0},{1,9},{9,1},{2,10},{10,2},{3,11},{11,3},{4,12},{12,4},... | collective-permute-start | bytes 1179656 | tf_op jit(solution)/shard_map/ppermute | solution.py:19
  204.7 18.9 %copy-start.1 = (bf16[1024,1536]{1,0:T(8,128)(2,1)S(1)}, bf16[1024,1536]{1,0:T(8,128)(2,1)}, u32[]{:S(2)}) copy-start(bf16[1024,1536]{1,0:T(8,128)(2,1)} %param.6) | copy-start | bytes 9437188
  207.7 10.9 %collective-permute-start.17 = (bf16[192,1024]{1,0:T(8,128)(2,1)}, bf16[192,1024]{1,0:T(8,128)(2,1)}, u32[]{:S(2)}, u32[]{:S(2)}) collective-permute-start(bf16[192,1024]{1,0:T(8,128)(2,1)} %slice.126), channel_id=1, source_target_pairs={{0,64},{64,0},{1,65},{65,1},{2,66},{66,2},{3,67},{67,3},{4,68},{68... | collective-permute-start | bytes 1179656 | tf_op jit(solution)/shard_map/ppermute | solution.py:19
  207.7 15.0 %copy-start.31 = (bf16[384,1024]{1,0:T(8,128)(2,1)S(1)}, bf16[384,1024]{1,0:T(8,128)(2,1)}, u32[]{:S(2)}) copy-start(bf16[384,1024]{1,0:T(8,128)(2,1)} %reduce-scatter.5.cloned.1.call-done) | copy-start | bytes 2359300
  208.8 13.8 %collective-permute-start.21 = (bf16[192,1024]{1,0:T(8,128)(2,1)S(1)}, bf16[192,1024]{1,0:T(8,128)(2,1)S(1)}, u32[]{:S(2)}, u32[]{:S(2)}) collective-permute-start(bf16[192,1024]{1,0:T(8,128)(2,1)S(1)} %slice.129), channel_id=1, source_target_pairs={{0,64},{64,0},{1,65},{65,1},{2,66},{66,2},{3,67},{67,3},{4,68},{68... | collective-permute-start | bytes 1179656 | tf_op jit(solution)/shard_map/ppermute | solution.py:19
  (33 other events, 125.8 us)
Sparse Core Ops, SparseCore 0:
  56.5 36.9 all-gather.1
  114.4 35.7 reduce-scatter.2
  152.6 37.9 reduce-scatter.4
where the time goes:
time: 232 us; the launch traced here: 230 us
  waiting for transfers between devices  77.2 us (33%)
  starting transfers between devices  50.8 us (22%)
  matrix products  34 us (15%)
  local copies, waits for them, and re-layouts  24.6 us (11%)
  other arithmetic  17.1 us (7%)
  between operations  14.3 us (6%)
  Pallas kernels  12.2 us (5%)
    ppermute x34, waiting for transfers between devices, shift(): lax.ppermute(value, axis, [(i, (i + step) % size) for i in range(size)])  71.9 us
    ppermute x34, starting transfers between devices, shift(): lax.ppermute(value, axis, [(i, (i + step) % size) for i in range(size)])  47.4 us
    dot_general x8, matrix products, dot(): return lax.dot_general(a, b, (dims, ((), ())), preferred_element_type=F32)  34 us
    unnamed x85, local copies, waits for them, and re-layouts  16.6 us
    pallas_call x2, Pallas kernels, place_rows(): pl.pallas_call(place_kernel, out_shape=jax.ShapeDtypeStruct((theirs.shape...  7.57 us
    ppermute x2, waiting for transfers between devices, y_step_down(): lax.ppermute(value, ('y_lo', 'y_hi'), [(at[y], at[(y + 3) % 4]) for y in...  5.23 us
  transfers between devices with their start and end apart: 39, of which 17 were waited for; matrix products, arithmetic and copies ran while one was open for 24% of the time, Pallas kernels for 5%

commit v1 on v0

--- a/solution.py
+++ b/solution.py
@@ -100,7 +100,7 @@
         in_specs=[scalars, scalars, whole, whole],
         out_specs=whole,
         scratch_shapes=[pltpu.VMEM((width, block_len), BF)],
-        compiler_params=pltpu.CompilerParams(vmem_limit_bytes=16 * 1024 * 1024),
+        compiler_params=pltpu.CompilerParams(vmem_limit_bytes=8 * 1024 * 1024),
         cost_estimate=pl.CostEstimate(flops=2000000, bytes_accessed=8000000, transcendentals=0),
     )(blocks, owners, cot_t, slot_weight)
 
@@ -129,7 +129,7 @@
         out_shape=jax.ShapeDtypeStruct((theirs.shape[0], count * block_len), BF),
         in_specs=[scalars, scalars, whole, whole, whole],
         out_specs=whole,
-        compiler_params=pltpu.CompilerParams(vmem_limit_bytes=24 * 1024 * 1024),
+        compiler_params=pltpu.CompilerParams(vmem_limit_bytes=12 * 1024 * 1024),
         cost_estimate=pl.CostEstimate(flops=3000000, bytes_accessed=9000000, transcendentals=0),
     )(slots, owners, mine, theirs, block_weight)
 
@@ -154,7 +154,7 @@
         out_shape=jax.ShapeDtypeStruct(tuple(shape), BF),
         in_specs=[whole] * len(pieces),
         out_specs=whole,
-        compiler_params=pltpu.CompilerParams(vmem_limit_bytes=16 * 1024 * 1024),
+        compiler_params=pltpu.CompilerParams(vmem_limit_bytes=8 * 1024 * 1024),
         cost_estimate=pl.CostEstimate(flops=0, bytes_accessed=6500000, transcendentals=0),
     )(*pieces)
 

time: 232 us -> 232 us (level)
  no operation moved by 1% of the time
where the time goes in v1:
time: 232 us; the launch traced here: 230 us
  waiting for transfers between devices  77.2 us (33%)
  starting transfers between devices  50.8 us (22%)
  matrix products  34 us (15%)
  local copies, waits for them, and re-layouts  24.6 us (11%)
  other arithmetic  17.1 us (7%)
  between operations  14.3 us (6%)
  Pallas kernels  12.2 us (5%)
    ppermute x34, waiting for transfers between devices, shift(): lax.ppermute(value, axis, [(i, (i + step) % size) for i in range(size)])  71.9 us
    ppermute x34, starting transfers between devices, shift(): lax.ppermute(value, axis, [(i, (i + step) % size) for i in range(size)])  47.4 us
    dot_general x8, matrix products, dot(): return lax.dot_general(a, b, (dims, ((), ())), preferred_element_type=F32)  34 us
    unnamed x85, local copies, waits for them, and re-layouts  16.6 us
    pallas_call x2, Pallas kernels, place_rows(): pl.pallas_call(place_kernel, out_shape=jax.ShapeDtypeStruct((theirs.shape...  7.57 us
    ppermute x2, waiting for transfers between devices, y_step_down(): lax.ppermute(value, ('y_lo', 'y_hi'), [(at[y], at[(y + 3) % 4]) for y in...  5.23 us
  transfers between devices with their start and end apart: 39, of which 17 were waited for; matrix products, arithmetic and copies ran while one was open for 24% of the time, Pallas kernels for 5%

profile of v1, /device:TPU:0, one launch (start us, length us, event | category | flops | bytes accessed | tf_op | source)
XLA Modules:
  0.0 230.1 jit_solution(9963985548083400094)
XLA Ops:
  9.5 2.1 gather_fusion
  11.5 3.3 %collective-permute-start.9 = (bf16[1536,128]{1,0:T(8,128)(2,1)S(1)}, bf16[1536,128]{1,0:T(8,128)(2,1)S(1)}, u32[]{:S(2)}, u32[]{:S(2)}) collective-permute-start(bf16[1536,128]{1,0:T(8,128)(2,1)S(1)} %bitcast.56), channel_id=1, source_target_pairs={{0,8},{8,0},{1,9},{9,1},{2,10},{10,2},{3,11},{11,3},{4,12},{12,4},... | collective-permute-start | bytes 1179656 | tf_op jit(solution)/shard_map/ppermute | solution.py:19
  14.8 1.9 collective-permute-start.10
  16.8 2.1 collective-permute-start.12
  19.9 4.7 %collective-permute-done.9.refs_1_ = bf16[1536,128]{1,0:T(8,128)(2,1)S(1)} collective-permute-done((bf16[1536,128]{1,0:T(8,128)(2,1)S(1)}, bf16[1536,128]{1,0:T(8,128)(2,1)S(1)}, u32[]{:S(2)}, u32[]{:S(2)}) %collective-permute-start.9) | collective-permute-done | bytes 393248 | tf_op jit(solution)/shard_map/ppermute | solution.py:19
  24.6 2.1 collective-permute-start.18
  28.7 2.9 %collective-permute-start.13 = (bf16[1536,128]{1,0:T(8,128)(2,1)S(1)}, bf16[1536,128]{1,0:T(8,128)(2,1)S(1)}, u32[]{:S(2)}, u32[]{:S(2)}) collective-permute-start(bf16[1536,128]{1,0:T(8,128)(2,1)S(1)} %collective-permute-done.9.refs_1_), channel_id=1, source_target_pairs={{0,6},{2,0},{4,2},{6,4},{1,7},{3,1},{5,3},{7,5},{8,14},{10,8},{12,... | collective-permute-start | bytes 1179656 | tf_op jit(solution)/shard_map/ppermute | solution.py:19
  31.6 2.3 %collective-permute-done = bf16[128,1536]{1,0:T(8,128)(2,1)S(1)} collective-permute-done((bf16[128,1536]{1,0:T(8,128)(2,1)}, bf16[128,1536]{1,0:T(8,128)(2,1)S(1)}, u32[]{:S(2)}, u32[]{:S(2)}) %collective-permute-start) | collective-permute-done | bytes 393248 | tf_op jit(solution)/shard_map/ppermute | solution.py:40
  33.9 2.2 collective-permute-start.1
  36.1 6.3 %collective-permute-done.18 = bf16[192,1024]{1,0:T(8,128)(2,1)S(1)} collective-permute-done((bf16[192,1024]{1,0:T(8,128)(2,1)}, bf16[192,1024]{1,0:T(8,128)(2,1)S(1)}, u32[]{:S(2)}, u32[]{:S(2)}) %collective-permute-start.18) | collective-permute-done | bytes 393248 | tf_op jit(solution)/shard_map/ppermute | solution.py:19
  42.4 1.9 collective-permute-start.11
  44.3 1.9 collective-permute-start.14
  47.5 2.9 %collective-permute-done.1.refs_1_ = bf16[128,1536]{1,0:T(8,128)(2,1)} collective-permute-done((bf16[128,1536]{1,0:T(8,128)(2,1)S(1)}, bf16[128,1536]{1,0:T(8,128)(2,1)}, u32[]{:S(2)}, u32[]{:S(2)}) %collective-permute-start.1) | collective-permute-done | bytes 393248 | tf_op jit(solution)/shard_map/ppermute | solution.py:40
  50.4 4.0 %collective-permute-start.5 = (bf16[128,1536]{1,0:T(8,128)(2,1)}, bf16[128,1536]{1,0:T(8,128)(2,1)}, u32[]{:S(2)}, u32[]{:S(2)}) collective-permute-start(bf16[128,1536]{1,0:T(8,128)(2,1)} %collective-permute-done.1.refs_1_), channel_id=1, source_target_pairs={{0,6},{2,0},{4,2},{6,4},{1,7},{3,1},{5,3},{7,5},{8,14},{10,8},{12,... | collective-permute-start | bytes 1179656 | tf_op jit(solution)/shard_map/ppermute | solution.py:19
  54.5 1.9 pad_maximum_fusion.2
  57.2 1.9 collective-permute-start.4
  59.1 4.2 %collective-permute-done.14.refs_6_ = bf16[1536,128]{1,0:T(8,128)(2,1)S(1)} collective-permute-done((bf16[1536,128]{1,0:T(8,128)(2,1)S(1)}, bf16[1536,128]{1,0:T(8,128)(2,1)S(1)}, u32[]{:S(2)}, u32[]{:S(2)}) %collective-permute-start.14) | collective-permute-done | bytes 393248 | tf_op jit(solution)/shard_map/ppermute | solution.py:19
  77.5 6.1 %collective-permute-done.3.refs_3_ = bf16[128,1536]{1,0:T(8,128)(2,1)S(1)} collective-permute-done((bf16[128,1536]{1,0:T(8,128)(2,1)}, bf16[128,1536]{1,0:T(8,128)(2,1)S(1)}, u32[]{:S(2)}, u32[]{:S(2)}) %collective-permute-start.3) | collective-permute-done | bytes 393248 | tf_op jit(solution)/shard_map/ppermute | solution.py:19
  85.0 2.9 %pad_maximum_fusion = bf16[1280,1536]{1,0:T(8,128)(2,1)S(1)} fusion(bf16[640,1536]{1,0:T(8,128)(2,1)} %collective-permute-done.8, bf16[640,1536]{1,0:T(8,128)(2,1)S(1)} %bitcast.65), kind=kLoop, calls=%fused_computation.12 | loop fusion | flops 7864320 | bytes 7864320 | tf_op jit(solution)/shard_map/concatenate | solution.py:201
  88.0 7.1 %fusion.4 = (bf16[1280,1024]{1,0:T(8,128)(2,1)}, bf16[1280,1024]{1,0:T(8,128)(2,1)S(1)}) fusion(bf16[1280,1536]{1,0:T(8,128)(2,1)S(1)} %pad_maximum_fusion, bf16[1536,1024]{1,0:T(8,128)(2,1)S(1)} %shard_map.94), kind=kOutput, calls=%fused_computation.8 | convolution fusion | flops 4040949760 | bytes 12320768 | tf_op jit(solution)/shard_map/dot_general | solution.py:75
  96.7 4.6 %convolution_convert_fusion.1.mine_ref = bf16[1536,1280]{1,0:T(8,128)(2,1)S(1)} fusion(bf16[1024,1536]{1,0:T(8,128)(2,1)S(1)} %shard_map.93, bf16[1280,1024]{1,0:T(8,128)(2,1)S(1)} %get-tuple-element.6), kind=kOutput, calls=%fused_computation.3 | convolution fusion | flops 4028497920 | bytes 9699328 | tf_op jit(solution)/shard_map/dot_general | solution.py:75
  102.7 1.9 copy-done.2
  105.1 1.9 copy-done.6
  107.0 2.2 shard_map.96
  109.9 4.3 %shard_map.95 = bf16[1536,1024]{1,0:T(8,128)(2,1)} custom-call(s32[8]{0:T(128)S(1)} %broadcast_minimum_fusion.slots_ref, s32[8]{0:T(128)S(1)} %fusion.15.owners_ref, bf16[1536,1280]{1,0:T(8,128)(2,1)S(1)} %copy-done.3, bf16[1536,640]{1,0:T(8,128)(2,1)} %collective-permute-done.16.theirs_ref, f32[8,1,128]{2,1,0:T(1,128)S(1)} %fusion.11.weight_ref), custom_call_target="tpu_custom_call" | custom-call | flops 3000000 | bytes 9000000 | tf_op jit(solution)/shard_map/pallas_call | solution.py:127
  114.3 2.0 pad_maximum_fusion.1
  117.6 4.6 %multiply_convert_fusion = bf16[1280,1024]{1,0:T(8,128)(2,1)S(1)} fusion(bf16[1280,1024]{1,0:T(8,128)(2,1)S(1)} %copy-done.41, bf16[1280,1536]{1,0:T(8,128)(2,1)S(1)} %pad_maximum_fusion.1, bf16[1024,1536]{1,0:T(8,128)(2,1)S(1)} %copy-done.8), kind=kOutput, calls=%fused_computation.9 | convolution fusion | flops 4030464000 | bytes 12320768 | tf_op jit(solution)/shard_map/dot_general | solution.py:75
  122.2 4.6 %convolution_convert_fusion.mine_ref = bf16[1536,1280]{1,0:T(8,128)(2,1)S(1)} fusion(bf16[1536,1024]{1,0:T(8,128)(2,1)S(1)} %copy-done.5, bf16[1280,1024]{1,0:T(8,128)(2,1)S(1)} %multiply_convert_fusion), kind=kOutput, calls=%fused_computation.2 | convolution fusion | flops 4028497920 | bytes 9699328 | tf_op jit(solution)/shard_map/dot_general | solution.py:75
  127.1 2.3 convolution_convert_fusion.4
  131.1 3.3 %shard_map.97 = bf16[1536,1024]{1,0:T(8,128)(2,1)} custom-call(s32[8]{0:T(128)S(1)} %broadcast_minimum_fusion.slots_ref, s32[8]{0:T(128)S(1)} %fusion.15.owners_ref, bf16[1536,1280]{1,0:T(8,128)(2,1)S(1)} %convolution_convert_fusion.mine_ref, bf16[1536,640]{1,0:T(8,128)(2,1)S(1)} %collective-permute-done.20.theirs_ref, ...), custom_call_target="tpu_custom_call" | custom-call | flops 3000000 | bytes 9000000 | tf_op jit(solution)/shard_map/pallas_call | solution.py:127
  134.6 3.2 %collective-permute-start.33 = (bf16[128,1536]{1,0:T(8,128)(2,1)S(1)}, bf16[128,1536]{1,0:T(8,128)(2,1)S(1)}, u32[]{:S(2)}, u32[]{:S(2)}) collective-permute-start(bf16[128,1536]{1,0:T(8,128)(2,1)S(1)} %get-tuple-element.21), channel_id=1, source_target_pairs={{0,6},{2,0},{4,2},{6,4},{1,7},{3,1},{5,3},{7,5},{8,14},{10,8},{12,... | collective-permute-start | bytes 1179656 | tf_op jit(solution)/shard_map/ppermute | solution.py:19
  137.8 6.0 %convolution_convert_fusion.2 = bf16[768,1536]{1,0:T(8,128)(2,1)S(1)} fusion(bf16[1280,1536]{1,0:T(8,128)(2,1)} %copy-done.28, bf16[1280,1024]{1,0:T(8,128)(2,1)} %copy-done.38), kind=kOutput, calls=%fused_computation.14 | convolution fusion | flops 3021078528 | bytes 8257536 | tf_op jit(solution)/shard_map/dot_general | solution.py:75
  144.0 3.2 %collective-permute-start.31 = (bf16[128,1536]{1,0:T(8,128)(2,1)S(1)}, bf16[128,1536]{1,0:T(8,128)(2,1)S(1)}, u32[]{:S(2)}, u32[]{:S(2)}) collective-permute-start(bf16[128,1536]{1,0:T(8,128)(2,1)S(1)} %get-tuple-element.14), channel_id=1, source_target_pairs={{0,6},{2,0},{4,2},{6,4},{1,7},{3,1},{5,3},{7,5},{8,14},{10,8},{12,... | collective-permute-start | bytes 1179656 | tf_op jit(solution)/shard_map/ppermute | solution.py:19
  148.8 3.6 %convolution_convert_fusion.3 = bf16[1536,768]{1,0:T(8,128)(2,1)S(1)} fusion(bf16[1280,1536]{1,0:T(8,128)(2,1)S(1)} %copy-done.27, bf16[1280,1024]{1,0:T(8,128)(2,1)S(1)} %copy-done.40), kind=kOutput, calls=%fused_computation.15 | convolution fusion | flops 3021078528 | bytes 8257536 | tf_op jit(solution)/shard_map/dot_general | solution.py:75
  153.3 3.2 %collective-permute-start.26 = (bf16[1536,128]{1,0:T(8,128)(2,1)S(1)}, bf16[1536,128]{1,0:T(8,128)(2,1)S(1)}, u32[]{:S(2)}, u32[]{:S(2)}) collective-permute-start(bf16[1536,128]{1,0:T(8,128)(2,1)S(1)} %get-tuple-element.23), channel_id=1, source_target_pairs={{0,6},{2,0},{4,2},{6,4},{1,7},{3,1},{5,3},{7,5},{8,14},{10,8},{12,... | collective-permute-start | bytes 1179656 | tf_op jit(solution)/shard_map/ppermute | solution.py:19
  156.7 8.9 %collective-permute-done.22 = bf16[1536,128]{1,0:T(8,128)(2,1)S(1)} collective-permute-done((bf16[1536,128]{1,0:T(8,128)(2,1)S(1)}, bf16[1536,128]{1,0:T(8,128)(2,1)S(1)}, u32[]{:S(2)}, u32[]{:S(2)}) %collective-permute-start.22) | collective-permute-done | bytes 393248 | tf_op jit(solution)/shard_map/ppermute | solution.py:19
  165.6 2.2 collective-permute-start.34
  168.7 14.7 %collective-permute-done.34 = bf16[128,1536]{1,0:T(8,128)(2,1)S(1)} collective-permute-done((bf16[128,1536]{1,0:T(8,128)(2,1)S(1)}, bf16[128,1536]{1,0:T(8,128)(2,1)S(1)}, u32[]{:S(2)}, u32[]{:S(2)}) %collective-permute-start.34) | collective-permute-done | bytes 393248 | tf_op jit(solution)/shard_map/ppermute | solution.py:19
  185.6 5.5 %collective-permute-done.27 = bf16[1536,128]{1,0:T(8,128)(2,1)S(1)} collective-permute-done((bf16[1536,128]{1,0:T(8,128)(2,1)S(1)}, bf16[1536,128]{1,0:T(8,128)(2,1)S(1)}, u32[]{:S(2)}, u32[]{:S(2)}) %collective-permute-start.27) | collective-permute-done | bytes 393248 | tf_op jit(solution)/shard_map/ppermute | solution.py:19
  191.2 1.8 collective-permute-start.35
  195.6 9.0 %collective-permute-done.35 = bf16[128,1536]{1,0:T(8,128)(2,1)S(1)} collective-permute-done((bf16[128,1536]{1,0:T(8,128)(2,1)S(1)}, bf16[128,1536]{1,0:T(8,128)(2,1)S(1)}, u32[]{:S(2)}, u32[]{:S(2)}) %collective-permute-start.35) | collective-permute-done | bytes 393248 | tf_op jit(solution)/shard_map/ppermute | solution.py:19
  205.7 1.9 slice.126
  208.8 2.1 collective-permute-start.21
  210.9 2.3 collective-permute-done.28
  213.2 2.3 add_bitcast_fusion.1
  215.5 3.1 %collective-permute-done.17 = bf16[192,1024]{1,0:T(8,128)(2,1)} collective-permute-done((bf16[192,1024]{1,0:T(8,128)(2,1)}, bf16[192,1024]{1,0:T(8,128)(2,1)}, u32[]{:S(2)}, u32[]{:S(2)}) %collective-permute-start.17) | collective-permute-done | bytes 393248 | tf_op jit(solution)/shard_map/ppermute | solution.py:19
  218.6 1.9 fusion.9
  220.4 2.2 collective-permute-done.21
  (165 shorter events, 42.3 us)
Async XLA Ops:
  7.2 97.9 %all-gather.2.cloned.1.call-start = ((), (), s32[]{:S(2)}) async-start(), calls=%async_computation.3 | async-start | bytes 3932160 | tf_op jit(solution)/shard_map/all_gather | solution.py:180
  11.5 73.5 %collective-permute-start.8 = (bf16[640,1536]{1,0:T(8,128)(2,1)}, bf16[640,1536]{1,0:T(8,128)(2,1)}, u32[]{:S(2)}, u32[]{:S(2)}) collective-permute-start(bf16[640,1536]{1,0:T(8,128)(2,1)} %bitcast.64), channel_id=1, source_target_pairs={{0,1},{1,0},{2,3},{3,2},{4,5},{5,4},{6,7},{7,6},{8,9},{9,8},{10,11... | collective-permute-start | bytes 5898248 | tf_op jit(solution)/shard_map/ppermute | solution.py:19
  11.5 13.1 %collective-permute-start.9 = (bf16[1536,128]{1,0:T(8,128)(2,1)S(1)}, bf16[1536,128]{1,0:T(8,128)(2,1)S(1)}, u32[]{:S(2)}, u32[]{:S(2)}) collective-permute-start(bf16[1536,128]{1,0:T(8,128)(2,1)S(1)} %bitcast.56), channel_id=1, source_target_pairs={{0,8},{8,0},{1,9},{9,1},{2,10},{10,2},{3,11},{11,3},{4,12},{12,4},... | collective-permute-start | bytes 1179656 | tf_op jit(solution)/shard_map/ppermute | solution.py:19
  14.8 13.5 %collective-permute-start.10 = (bf16[1536,128]{1,0:T(8,128)(2,1)S(1)}, bf16[1536,128]{1,0:T(8,128)(2,1)S(1)}, u32[]{:S(2)}, u32[]{:S(2)}) collective-permute-start(bf16[1536,128]{1,0:T(8,128)(2,1)S(1)} %bitcast.57), channel_id=1, source_target_pairs={{0,2},{2,4},{4,6},{6,0},{1,3},{3,5},{5,7},{7,1},{8,10},{10,12},{12... | collective-permute-start | bytes 1179656 | tf_op jit(solution)/shard_map/ppermute | solution.py:19
  16.8 11.9 %collective-permute-start.12 = (bf16[1536,128]{1,0:T(8,128)(2,1)S(1)}, bf16[1536,128]{1,0:T(8,128)(2,1)S(1)}, u32[]{:S(2)}, u32[]{:S(2)}) collective-permute-start(bf16[1536,128]{1,0:T(8,128)(2,1)S(1)} %bitcast.58), channel_id=1, source_target_pairs={{0,6},{2,0},{4,2},{6,4},{1,7},{3,1},{5,3},{7,5},{8,14},{10,8},{12,... | collective-permute-start | bytes 1179656 | tf_op jit(solution)/shard_map/ppermute | solution.py:19
  18.9 15.1 %collective-permute-start = (bf16[128,1536]{1,0:T(8,128)(2,1)}, bf16[128,1536]{1,0:T(8,128)(2,1)S(1)}, u32[]{:S(2)}, u32[]{:S(2)}) collective-permute-start(bf16[128,1536]{1,0:T(8,128)(2,1)} %bitcast.60), channel_id=1, source_target_pairs={{0,72},{64,0},{8,64},{72,8},{1,73},{65,1},{9,65},{73,9},{2,74},{66... | collective-permute-start | bytes 1179656 | tf_op jit(solution)/shard_map/ppermute | solution.py:40
  24.6 42.1 %copy-start.11 = (bf16[1536,128]{1,0:T(8,128)(2,1)}, bf16[1536,128]{1,0:T(8,128)(2,1)S(1)}, u32[]{:S(2)}) copy-start(bf16[1536,128]{1,0:T(8,128)(2,1)S(1)} %collective-permute-done.9.refs_1_) | copy-start | bytes 1179652
  24.6 17.7 %collective-permute-start.18 = (bf16[192,1024]{1,0:T(8,128)(2,1)}, bf16[192,1024]{1,0:T(8,128)(2,1)S(1)}, u32[]{:S(2)}, u32[]{:S(2)}) collective-permute-start(bf16[192,1024]{1,0:T(8,128)(2,1)} %bitcast.66), channel_id=1, source_target_pairs={{0,64},{64,0},{1,65},{65,1},{2,66},{66,2},{3,67},{67,3},{4,68},{68... | collective-permute-start | bytes 1179656 | tf_op jit(solution)/shard_map/ppermute | solution.py:19
  28.4 38.4 %copy-start.13 = (bf16[1536,128]{1,0:T(8,128)(2,1)}, bf16[1536,128]{1,0:T(8,128)(2,1)S(1)}, u32[]{:S(2)}) copy-start(bf16[1536,128]{1,0:T(8,128)(2,1)S(1)} %collective-permute-done.10.refs_2_) | copy-start | bytes 1179652
  28.4 15.9 %collective-permute-start.2 = (bf16[128,1536]{1,0:T(8,128)(2,1)}, bf16[128,1536]{1,0:T(8,128)(2,1)}, u32[]{:S(2)}, u32[]{:S(2)}) collective-permute-start(bf16[128,1536]{1,0:T(8,128)(2,1)} %bitcast.61), channel_id=1, source_target_pairs={{0,2},{2,4},{4,6},{6,0},{1,3},{3,5},{5,7},{7,1},{8,10},{10,12},{12... | collective-permute-start | bytes 1179656 | tf_op jit(solution)/shard_map/ppermute | solution.py:19
  28.7 38.1 %copy-start.15 = (bf16[1536,128]{1,0:T(8,128)(2,1)}, bf16[1536,128]{1,0:T(8,128)(2,1)S(1)}, u32[]{:S(2)}) copy-start(bf16[1536,128]{1,0:T(8,128)(2,1)S(1)} %collective-permute-done.12.refs_4_) | copy-start | bytes 1179652
  28.7 17.5 %collective-permute-start.13 = (bf16[1536,128]{1,0:T(8,128)(2,1)S(1)}, bf16[1536,128]{1,0:T(8,128)(2,1)S(1)}, u32[]{:S(2)}, u32[]{:S(2)}) collective-permute-start(bf16[1536,128]{1,0:T(8,128)(2,1)S(1)} %collective-permute-done.9.refs_1_), channel_id=1, source_target_pairs={{0,6},{2,0},{4,2},{6,4},{1,7},{3,1},{5,3},{7,5},{8,14},{10,8},{12,... | collective-permute-start | bytes 1179656 | tf_op jit(solution)/shard_map/ppermute | solution.py:19
  33.9 16.5 %collective-permute-start.1 = (bf16[128,1536]{1,0:T(8,128)(2,1)S(1)}, bf16[128,1536]{1,0:T(8,128)(2,1)}, u32[]{:S(2)}, u32[]{:S(2)}) collective-permute-start(bf16[128,1536]{1,0:T(8,128)(2,1)S(1)} %collective-permute-done), channel_id=1, source_target_pairs={{0,72},{64,0},{8,64},{72,8},{1,73},{65,1},{9,65},{73,9},{2,74},{66... | collective-permute-start | bytes 1179656 | tf_op jit(solution)/shard_map/ppermute | solution.py:40
  42.4 14.1 %collective-permute-start.11 = (bf16[1536,128]{1,0:T(8,128)(2,1)S(1)}, bf16[1536,128]{1,0:T(8,128)(2,1)S(1)}, u32[]{:S(2)}, u32[]{:S(2)}) collective-permute-start(bf16[1536,128]{1,0:T(8,128)(2,1)S(1)} %collective-permute-done.9.refs_1_), channel_id=1, source_target_pairs={{0,2},{2,4},{4,6},{6,0},{1,3},{3,5},{5,7},{7,1},{8,10},{10,12},{12... | collective-permute-start | bytes 1179656 | tf_op jit(solution)/shard_map/ppermute | solution.py:19
  44.3 19.0 %collective-permute-start.14 = (bf16[1536,128]{1,0:T(8,128)(2,1)S(1)}, bf16[1536,128]{1,0:T(8,128)(2,1)S(1)}, u32[]{:S(2)}, u32[]{:S(2)}) collective-permute-start(bf16[1536,128]{1,0:T(8,128)(2,1)S(1)} %collective-permute-done.10.refs_2_), channel_id=1, source_target_pairs={{0,2},{2,4},{4,6},{6,0},{1,3},{3,5},{5,7},{7,1},{8,10},{10,12},{12... | collective-permute-start | bytes 1179656 | tf_op jit(solution)/shard_map/ppermute | solution.py:19
  46.2 20.5 %copy-start.17 = (bf16[1536,128]{1,0:T(8,128)(2,1)}, bf16[1536,128]{1,0:T(8,128)(2,1)S(1)}, u32[]{:S(2)}) copy-start(bf16[1536,128]{1,0:T(8,128)(2,1)S(1)} %collective-permute-done.13.refs_5_) | copy-start | bytes 1179652
  46.2 17.8 %collective-permute-start.15 = (bf16[1536,128]{1,0:T(8,128)(2,1)S(1)}, bf16[1536,128]{1,0:T(8,128)(2,1)S(1)}, u32[]{:S(2)}, u32[]{:S(2)}) collective-permute-start(bf16[1536,128]{1,0:T(8,128)(2,1)S(1)} %collective-permute-done.13.refs_5_), channel_id=1, source_target_pairs={{0,6},{2,0},{4,2},{6,4},{1,7},{3,1},{5,3},{7,5},{8,14},{10,8},{12,... | collective-permute-start | bytes 1179656 | tf_op jit(solution)/shard_map/ppermute | solution.py:19
  50.4 16.3 %collective-permute-start.5 = (bf16[128,1536]{1,0:T(8,128)(2,1)}, bf16[128,1536]{1,0:T(8,128)(2,1)}, u32[]{:S(2)}, u32[]{:S(2)}) collective-permute-start(bf16[128,1536]{1,0:T(8,128)(2,1)} %collective-permute-done.1.refs_1_), channel_id=1, source_target_pairs={{0,6},{2,0},{4,2},{6,4},{1,7},{3,1},{5,3},{7,5},{8,14},{10,8},{12,... | collective-permute-start | bytes 1179656 | tf_op jit(solution)/shard_map/ppermute | solution.py:19
  56.4 149.3 %reduce-scatter.3.cloned.1.call-start = ((), (), s32[]{:S(2)}) async-start(), calls=%async_computation.2 | async-start | bytes 3932160 | tf_op jit(solution)/shard_map/reduce_scatter | solution.py:231
  56.5 27.1 %copy-start.10 = (bf16[1,128,1536]{2,1,0:T(8,128)(2,1)S(1)}, bf16[1,128,1536]{2,1,0:T(8,128)(2,1)}, u32[]{:S(2)}) copy-start(bf16[1,128,1536]{2,1,0:T(8,128)(2,1)} %param.11) | copy-start | bytes 1179652
  57.2 18.8 %collective-permute-start.4 = (bf16[128,1536]{1,0:T(8,128)(2,1)}, bf16[128,1536]{1,0:T(8,128)(2,1)S(1)}, u32[]{:S(2)}, u32[]{:S(2)}) collective-permute-start(bf16[128,1536]{1,0:T(8,128)(2,1)} %bitcast.62), channel_id=1, source_target_pairs={{0,6},{2,0},{4,2},{6,4},{1,7},{3,1},{5,3},{7,5},{8,14},{10,8},{12,... | collective-permute-start | bytes 1179656 | tf_op jit(solution)/shard_map/ppermute | solution.py:19
  64.0 13.4 %collective-permute-start.6 = (bf16[128,1536]{1,0:T(8,128)(2,1)}, bf16[128,1536]{1,0:T(8,128)(2,1)S(1)}, u32[]{:S(2)}, u32[]{:S(2)}) collective-permute-start(bf16[128,1536]{1,0:T(8,128)(2,1)} %collective-permute-done.2.refs_2_), channel_id=1, source_target_pairs={{0,2},{2,4},{4,6},{6,0},{1,3},{3,5},{5,7},{7,1},{8,10},{10,12},{12... | collective-permute-start | bytes 1179656 | tf_op jit(solution)/shard_map/ppermute | solution.py:19
  64.8 18.7 %collective-permute-start.3 = (bf16[128,1536]{1,0:T(8,128)(2,1)}, bf16[128,1536]{1,0:T(8,128)(2,1)S(1)}, u32[]{:S(2)}, u32[]{:S(2)}) collective-permute-start(bf16[128,1536]{1,0:T(8,128)(2,1)} %collective-permute-done.1.refs_1_), channel_id=1, source_target_pairs={{0,2},{2,4},{4,6},{6,0},{1,3},{3,5},{5,7},{7,1},{8,10},{10,12},{12... | collective-permute-start | bytes 1179656 | tf_op jit(solution)/shard_map/ppermute | solution.py:19
  66.8 16.8 %collective-permute-start.7 = (bf16[128,1536]{1,0:T(8,128)(2,1)}, bf16[128,1536]{1,0:T(8,128)(2,1)S(1)}, u32[]{:S(2)}, u32[]{:S(2)}) collective-permute-start(bf16[128,1536]{1,0:T(8,128)(2,1)} %collective-permute-done.5.refs_5_), channel_id=1, source_target_pairs={{0,6},{2,0},{4,2},{6,4},{1,7},{3,1},{5,3},{7,5},{8,14},{10,8},{12,... | collective-permute-start | bytes 1179656 | tf_op jit(solution)/shard_map/ppermute | solution.py:19
  104.7 5.3 %collective-permute-start.16 = (bf16[1536,640]{1,0:T(8,128)(2,1)}, bf16[1536,640]{1,0:T(8,128)(2,1)}, u32[]{:S(2)}, u32[]{:S(2)}) collective-permute-start(bf16[1536,640]{1,0:T(8,128)(2,1)} %slice.122), channel_id=1, source_target_pairs={{0,1},{1,0},{2,3},{3,2},{4,5},{5,4},{6,7},{7,6},{8,9},{9,8},{10,11... | collective-permute-start | bytes 5898248 | tf_op jit(solution)/shard_map/ppermute | solution.py:19
  109.2 5.1 %collective-permute-start.19 = (bf16[640,1536]{1,0:T(8,128)(2,1)S(1)}, bf16[640,1536]{1,0:T(8,128)(2,1)}, u32[]{:S(2)}, u32[]{:S(2)}) collective-permute-start(bf16[640,1536]{1,0:T(8,128)(2,1)S(1)} %shard_map.96), channel_id=1, source_target_pairs={{0,1},{1,0},{2,3},{3,2},{4,5},{5,4},{6,7},{7,6},{8,9},{9,8},{10,11... | collective-permute-start | bytes 5898248 | tf_op jit(solution)/shard_map/ppermute | solution.py:19
  114.2 93.4 %reduce-scatter.5.cloned.1.call-start = ((), (), s32[]{:S(2)}) async-start(), calls=%async_computation.4 | async-start | bytes 3932160 | tf_op jit(solution)/shard_map/reduce_scatter | solution.py:231
  127.0 4.1 %collective-permute-start.20 = (bf16[1536,640]{1,0:T(8,128)(2,1)S(1)}, bf16[1536,640]{1,0:T(8,128)(2,1)S(1)}, u32[]{:S(2)}, u32[]{:S(2)}) collective-permute-start(bf16[1536,640]{1,0:T(8,128)(2,1)S(1)} %slice.127), channel_id=1, source_target_pairs={{0,1},{1,0},{2,3},{3,2},{4,5},{5,4},{6,7},{7,6},{8,9},{9,8},{10,11... | collective-permute-start | bytes 5898248 | tf_op jit(solution)/shard_map/ppermute | solution.py:19
  134.5 18.8 %collective-permute-start.29 = (bf16[128,1536]{1,0:T(8,128)(2,1)S(1)}, bf16[128,1536]{1,0:T(8,128)(2,1)S(1)}, u32[]{:S(2)}, u32[]{:S(2)}) collective-permute-start(bf16[128,1536]{1,0:T(8,128)(2,1)S(1)} %get-tuple-element.20), channel_id=1, source_target_pairs={{0,2},{2,4},{4,6},{6,0},{1,3},{3,5},{5,7},{7,1},{8,10},{10,12},{12... | collective-permute-start | bytes 1179656 | tf_op jit(solution)/shard_map/ppermute | solution.py:19
  134.6 12.6 %copy-start.27 = (bf16[1280,1536]{1,0:T(8,128)(2,1)S(1)}, bf16[1280,1536]{1,0:T(8,128)(2,1)}, u32[]{:S(2)}) copy-start(bf16[1280,1536]{1,0:T(8,128)(2,1)} %copy-done.26) | copy-start | bytes 11796484
  134.6 21.9 %collective-permute-start.33 = (bf16[128,1536]{1,0:T(8,128)(2,1)S(1)}, bf16[128,1536]{1,0:T(8,128)(2,1)S(1)}, u32[]{:S(2)}, u32[]{:S(2)}) collective-permute-start(bf16[128,1536]{1,0:T(8,128)(2,1)S(1)} %get-tuple-element.21), channel_id=1, source_target_pairs={{0,6},{2,0},{4,2},{6,4},{1,7},{3,1},{5,3},{7,5},{8,14},{10,8},{12,... | collective-permute-start | bytes 1179656 | tf_op jit(solution)/shard_map/ppermute | solution.py:19
  143.9 24.8 %collective-permute-start.32 = (bf16[128,1536]{1,0:T(8,128)(2,1)S(1)}, bf16[128,1536]{1,0:T(8,128)(2,1)S(1)}, u32[]{:S(2)}, u32[]{:S(2)}) collective-permute-start(bf16[128,1536]{1,0:T(8,128)(2,1)S(1)} %get-tuple-element.15), channel_id=1, source_target_pairs={{0,2},{2,4},{4,6},{6,0},{1,3},{3,5},{5,7},{7,1},{8,10},{10,12},{12... | collective-permute-start | bytes 1179656 | tf_op jit(solution)/shard_map/ppermute | solution.py:19
  144.0 50.0 %collective-permute-start.31 = (bf16[128,1536]{1,0:T(8,128)(2,1)S(1)}, bf16[128,1536]{1,0:T(8,128)(2,1)S(1)}, u32[]{:S(2)}, u32[]{:S(2)}) collective-permute-start(bf16[128,1536]{1,0:T(8,128)(2,1)S(1)} %get-tuple-element.14), channel_id=1, source_target_pairs={{0,6},{2,0},{4,2},{6,4},{1,7},{3,1},{5,3},{7,5},{8,14},{10,8},{12,... | collective-permute-start | bytes 1179656 | tf_op jit(solution)/shard_map/ppermute | solution.py:19
  148.5 17.1 %collective-permute-start.22 = (bf16[1536,128]{1,0:T(8,128)(2,1)S(1)}, bf16[1536,128]{1,0:T(8,128)(2,1)S(1)}, u32[]{:S(2)}, u32[]{:S(2)}) collective-permute-start(bf16[1536,128]{1,0:T(8,128)(2,1)S(1)} %get-tuple-element.22), channel_id=1, source_target_pairs={{0,2},{2,4},{4,6},{6,0},{1,3},{3,5},{5,7},{7,1},{8,10},{10,12},{12... | collective-permute-start | bytes 1179656 | tf_op jit(solution)/shard_map/ppermute | solution.py:19
  152.4 40.6 %copy-start.29 = (bf16[1536,768]{1,0:T(8,128)(2,1)}, bf16[1536,768]{1,0:T(8,128)(2,1)S(1)}, u32[]{:S(2)}) copy-start(bf16[1536,768]{1,0:T(8,128)(2,1)S(1)} %convolution_convert_fusion.3) | copy-start | bytes 7077892
  153.3 12.3 %collective-permute-start.26 = (bf16[1536,128]{1,0:T(8,128)(2,1)S(1)}, bf16[1536,128]{1,0:T(8,128)(2,1)S(1)}, u32[]{:S(2)}, u32[]{:S(2)}) collective-permute-start(bf16[1536,128]{1,0:T(8,128)(2,1)S(1)} %get-tuple-element.23), channel_id=1, source_target_pairs={{0,6},{2,0},{4,2},{6,4},{1,7},{3,1},{5,3},{7,5},{8,14},{10,8},{12,... | collective-permute-start | bytes 1179656 | tf_op jit(solution)/shard_map/ppermute | solution.py:19
  156.5 28.0 %collective-permute-start.25 = (bf16[1536,128]{1,0:T(8,128)(2,1)S(1)}, bf16[1536,128]{1,0:T(8,128)(2,1)S(1)}, u32[]{:S(2)}, u32[]{:S(2)}) collective-permute-start(bf16[1536,128]{1,0:T(8,128)(2,1)S(1)} %get-tuple-element.19), channel_id=1, source_target_pairs={{0,2},{2,4},{4,6},{6,0},{1,3},{3,5},{5,7},{7,1},{8,10},{10,12},{12... | collective-permute-start | bytes 1179656 | tf_op jit(solution)/shard_map/ppermute | solution.py:19
  165.6 45.3 %collective-permute-start.24 = (bf16[1536,128]{1,0:T(8,128)(2,1)}, bf16[1536,128]{1,0:T(8,128)(2,1)S(1)}, u32[]{:S(2)}, u32[]{:S(2)}) collective-permute-start(bf16[1536,128]{1,0:T(8,128)(2,1)} %get-tuple-element.18), channel_id=1, source_target_pairs={{0,6},{2,0},{4,2},{6,4},{1,7},{3,1},{5,3},{7,5},{8,14},{10,8},{12,... | collective-permute-start | bytes 1179656 | tf_op jit(solution)/shard_map/ppermute | solution.py:19
  165.6 17.8 %collective-permute-start.34 = (bf16[128,1536]{1,0:T(8,128)(2,1)S(1)}, bf16[128,1536]{1,0:T(8,128)(2,1)S(1)}, u32[]{:S(2)}, u32[]{:S(2)}) collective-permute-start(bf16[128,1536]{1,0:T(8,128)(2,1)S(1)} %get-tuple-element.13), channel_id=1, source_target_pairs={{0,6},{2,0},{4,2},{6,4},{1,7},{3,1},{5,3},{7,5},{8,14},{10,8},{12,... | collective-permute-start | bytes 1179656 | tf_op jit(solution)/shard_map/ppermute | solution.py:19
  168.7 26.9 %collective-permute-start.30 = (bf16[128,1536]{1,0:T(8,128)(2,1)S(1)}, bf16[128,1536]{1,0:T(8,128)(2,1)S(1)}, u32[]{:S(2)}, u32[]{:S(2)}) collective-permute-start(bf16[128,1536]{1,0:T(8,128)(2,1)S(1)} %get-tuple-element.12), channel_id=1, source_target_pairs={{0,2},{2,4},{4,6},{6,0},{1,3},{3,5},{5,7},{7,1},{8,10},{10,12},{12... | collective-permute-start | bytes 1179656 | tf_op jit(solution)/shard_map/ppermute | solution.py:19
  183.4 7.8 %collective-permute-start.27 = (bf16[1536,128]{1,0:T(8,128)(2,1)S(1)}, bf16[1536,128]{1,0:T(8,128)(2,1)S(1)}, u32[]{:S(2)}, u32[]{:S(2)}) collective-permute-start(bf16[1536,128]{1,0:T(8,128)(2,1)S(1)} %get-tuple-element.17), channel_id=1, source_target_pairs={{0,6},{2,0},{4,2},{6,4},{1,7},{3,1},{5,3},{7,5},{8,14},{10,8},{12,... | collective-permute-start | bytes 1179656 | tf_op jit(solution)/shard_map/ppermute | solution.py:19
  184.5 26.4 %collective-permute-start.23 = (bf16[1536,128]{1,0:T(8,128)(2,1)}, bf16[1536,128]{1,0:T(8,128)(2,1)}, u32[]{:S(2)}, u32[]{:S(2)}) collective-permute-start(bf16[1536,128]{1,0:T(8,128)(2,1)} %get-tuple-element.16), channel_id=1, source_target_pairs={{0,2},{2,4},{4,6},{6,0},{1,3},{3,5},{5,7},{7,1},{8,10},{10,12},{12... | collective-permute-start | bytes 1179656 | tf_op jit(solution)/shard_map/ppermute | solution.py:19
  191.2 13.5 %collective-permute-start.35 = (bf16[128,1536]{1,0:T(8,128)(2,1)S(1)}, bf16[128,1536]{1,0:T(8,128)(2,1)S(1)}, u32[]{:S(2)}, u32[]{:S(2)}) collective-permute-start(bf16[128,1536]{1,0:T(8,128)(2,1)S(1)} %add_convert_fusion), channel_id=1, source_target_pairs={{0,8},{8,0},{1,9},{9,1},{2,10},{10,2},{3,11},{11,3},{4,12},{12,4},... | collective-permute-start | bytes 1179656 | tf_op jit(solution)/shard_map/ppermute | solution.py:19
  193.9 19.3 %collective-permute-start.28 = (bf16[1536,128]{1,0:T(8,128)(2,1)}, bf16[1536,128]{1,0:T(8,128)(2,1)}, u32[]{:S(2)}, u32[]{:S(2)}) collective-permute-start(bf16[1536,128]{1,0:T(8,128)(2,1)} %add_convert_fusion.3), channel_id=1, source_target_pairs={{0,8},{8,0},{1,9},{9,1},{2,10},{10,2},{3,11},{11,3},{4,12},{12,4},... | collective-permute-start | bytes 1179656 | tf_op jit(solution)/shard_map/ppermute | solution.py:19
  204.7 18.9 %copy-start.1 = (bf16[1024,1536]{1,0:T(8,128)(2,1)S(1)}, bf16[1024,1536]{1,0:T(8,128)(2,1)}, u32[]{:S(2)}) copy-start(bf16[1024,1536]{1,0:T(8,128)(2,1)} %param.6) | copy-start | bytes 9437188
  207.7 10.9 %collective-permute-start.17 = (bf16[192,1024]{1,0:T(8,128)(2,1)}, bf16[192,1024]{1,0:T(8,128)(2,1)}, u32[]{:S(2)}, u32[]{:S(2)}) collective-permute-start(bf16[192,1024]{1,0:T(8,128)(2,1)} %slice.126), channel_id=1, source_target_pairs={{0,64},{64,0},{1,65},{65,1},{2,66},{66,2},{3,67},{67,3},{4,68},{68... | collective-permute-start | bytes 1179656 | tf_op jit(solution)/shard_map/ppermute | solution.py:19
  207.7 15.0 %copy-start.31 = (bf16[384,1024]{1,0:T(8,128)(2,1)S(1)}, bf16[384,1024]{1,0:T(8,128)(2,1)}, u32[]{:S(2)}) copy-start(bf16[384,1024]{1,0:T(8,128)(2,1)} %reduce-scatter.5.cloned.1.call-done) | copy-start | bytes 2359300
  208.8 13.8 %collective-permute-start.21 = (bf16[192,1024]{1,0:T(8,128)(2,1)S(1)}, bf16[192,1024]{1,0:T(8,128)(2,1)S(1)}, u32[]{:S(2)}, u32[]{:S(2)}) collective-permute-start(bf16[192,1024]{1,0:T(8,128)(2,1)S(1)} %slice.129), channel_id=1, source_target_pairs={{0,64},{64,0},{1,65},{65,1},{2,66},{66,2},{3,67},{67,3},{4,68},{68... | collective-permute-start | bytes 1179656 | tf_op jit(solution)/shard_map/ppermute | solution.py:19
  (33 other events, 125.8 us)
Sparse Core Ops, SparseCore 0:
  56.5 36.9 all-gather.1
  114.4 35.7 reduce-scatter.2
  152.6 37.9 reduce-scatter.4
